TPU v7x, 768 devices: a whole 4x8x12 slice. The times are simulated.
768 devices in a mesh: sample: 24 (over x, z_lo, core), chan: 32 (over z_hi, y).
Axes of the slice: x: 4, y: 8, z: 12 (z_hi: 4, z_lo: 3; z = z_hi * 3 + z_lo), core: 2. Of those that a mesh axis runs over, the one named last changes fastest.
Arguments:
- act_64: bfloat16 [24, 64, 8, 8, 256], P('sample'), may hold values from -6 to 6
- cot_32: bfloat16 [24, 32, 4, 4, 512], P('sample', None, None, None, 'chan'), may hold values from -2.5 to 2.5
- filters_32: bfloat16 [3, 3, 3, 256, 512], P(None, None, None, None, 'chan'), may hold values from -0.078125 to 0.078125
- act_128: bfloat16 [24, 128, 16, 16, 128], P('sample', 'chan'), may hold values from -6 to 6
Outputs:
- grad_filters_32: float32 [3, 3, 3, 256, 512], P(None, None, None, None, 'chan')
- grad_filters_64: float32 [3, 3, 3, 128, 256], P(None, None, None, 'chan')
- cot_64: float32 [24, 64, 8, 8, 256], P('sample', 'chan')
All inputs are finite; a program needn't handle non-finite values.
Results may differ from a plain program's by a relative error of at most 0.0029.
Values may be sent and summed in bfloat16 or wider, within the bound.
A program may use at most 64 MiB of HBM per device.

v0:
```python
import jax
import jax.numpy as jnp
from jax import lax
from jax.sharding import PartitionSpec as P

leak_slope = 0.3


def passed_along(array, axis, by):
    size = lax.axis_size(axis)
    pairs = [(i, i + by) for i in range(size) if 0 <= i + by < size]
    return lax.ppermute(array, axis, pairs)


def tap_stack(padded_grid, depth, height, width):
    tap_list = []
    for depth_tap in range(3):
        for row_tap in range(3):
            for col_tap in range(3):
                window = padded_grid[
                    depth_tap : depth_tap + 2 * depth : 2,
                    row_tap : row_tap + 2 * height : 2,
                    col_tap : col_tap + 2 * width : 2,
                ]
                tap_list.append(window.reshape(depth * height * width, padded_grid.shape[3]))
    return jnp.stack(tap_list)


def spread(extended, filters):
    depth = extended.shape[0] - 1
    height = extended.shape[1] - 1
    width = extended.shape[2] - 1
    parity_taps = (((1, 0),), ((2, 0), (0, 1)))
    classes = []
    for depth_par in range(2):
        for row_par in range(2):
            for col_par in range(2):
                lefts = []
                rights = []
                for depth_tap, depth_off in parity_taps[depth_par]:
                    for row_tap, row_off in parity_taps[row_par]:
                        for col_tap, col_off in parity_taps[col_par]:
                            lefts.append(
                                extended[
                                    depth_off : depth_off + depth,
                                    row_off : row_off + height,
                                    col_off : col_off + width,
                                ]
                            )
                            rights.append(filters[depth_tap, row_tap, col_tap])
                left_side = jnp.concatenate(lefts, axis=3)
                right_side = jnp.concatenate(rights, axis=1)
                classes.append(
                    jnp.einsum(
                        "zyxf,cf->zyxc", left_side, right_side, preferred_element_type=jnp.float32
                    )
                )
    stacked = jnp.stack(classes).reshape(2, 2, 2, depth, height, width, filters.shape[3])
    return stacked.transpose(3, 0, 4, 1, 5, 2, 6).reshape(
        2 * depth, 2 * height, 2 * width, filters.shape[3]
    )


def body(act_64, cot_32, filters_32, act_128):
    shards = lax.axis_size("chan")
    volume_64 = act_64[0]
    cot_local = cot_32[0]
    depth, height, width, shard_out = cot_local.shape
    padded_64 = jnp.pad(volume_64, ((1, 1), (1, 1), (1, 1), (0, 0)))
    upper_terms = []
    for depth_tap in range(3):
        for row_tap in range(3):
            for col_tap in range(3):
                window = padded_64[
                    depth_tap : depth_tap + 2 * depth : 2,
                    row_tap : row_tap + 2 * height : 2,
                    col_tap : col_tap + 2 * width : 2,
                ]
                upper_terms.append(
                    jnp.einsum(
                        "zyxc,zyxf->cf", window, cot_local, preferred_element_type=jnp.float32
                    )
                )
    grad_upper = jnp.stack(upper_terms).reshape(filters_32.shape)
    slab_depth = volume_64.shape[0] // shards
    extended = jnp.pad(cot_local, ((0, 1), (0, 1), (0, 1), (0, 0)))
    partial_64 = spread(extended, filters_32)
    grad_64 = lax.psum_scatter(partial_64, "chan", scatter_dimension=0, tiled=True)
    own_volume = lax.dynamic_slice_in_dim(
        volume_64, lax.axis_index("chan") * slab_depth, slab_depth, 0
    )
    cot_full = grad_64 * jnp.where(own_volume > 0, 1.0, leak_slope)
    cot_lower = cot_full.astype(jnp.bfloat16)
    lower_rim = passed_along(act_128[:, -1:], "chan", 1)
    lower_window = jnp.concatenate([lower_rim, act_128], axis=1)[0]
    padded_128 = jnp.pad(lower_window, ((0, 0), (1, 1), (1, 1), (0, 0)))
    lower_taps = tap_stack(padded_128, slab_depth, 2 * height, 2 * width)
    grad_lower = jnp.einsum(
        "tpc,pf->tcf",
        lower_taps,
        cot_lower.reshape(-1, cot_lower.shape[3]),
        preferred_element_type=jnp.float32,
    )
    grad_lower = grad_lower.reshape(3, 3, 3, act_128.shape[4], cot_lower.shape[3])
    lower_share = lax.psum_scatter(grad_lower, "chan", scatter_dimension=3, tiled=True)
    total_upper, total_lower = lax.psum((grad_upper, lower_share), "sample")
    samples = lax.axis_size("sample")
    return (total_upper / samples, total_lower / samples, cot_full[None])


def solution(mesh):
    placed = (
        P("sample", None, None, None, None),
        P("sample", None, None, None, "chan"),
        P(None, None, None, None, "chan"),
        P("sample", "chan", None, None, None),
    )
    return jax.shard_map(
        body,
        mesh=mesh,
        in_specs=placed,
        out_specs=(
            P(None, None, None, None, "chan"),
            P(None, None, None, "chan", None),
            P("sample", "chan", None, None, None),
        ),
        check_vma=False,
    )
```

profile of v0, /device:TPU:208, one launch (start us, length us, event | category | flops | bytes accessed | tf_op | source)
XLA Modules:
  0.0 915.9 jit_solution(12834349501441058084)
XLA Ops:
  9.0 1.9 fusion
  21.3 7.4 copy.138
  28.7 6.1 reshape.28
  36.5 3.7 collective-permute-start
  41.3 3.2 pad.12
  44.6 8.8 slice.287
  53.3 8.8 slice.288
  62.1 8.8 slice.289
  70.9 8.8 slice.290
  79.6 8.8 slice.291
  88.4 8.8 slice.292
  97.2 7.0 slice.293
  104.2 7.1 slice.294
  111.3 7.1 slice.295
  118.4 7.0 slice.296
  125.4 7.1 slice.297
  147.9 7.0 slice.298
  156.1 4.7 slice.315
  160.9 4.8 slice.316
  165.6 4.8 slice.317
  170.4 4.7 slice.318
  175.1 4.7 slice.319
  179.8 4.8 slice.320
  184.6 4.7 slice.321
  189.3 4.8 slice.322
  194.1 4.8 slice.323
  198.9 4.7 slice.324
  203.6 4.8 slice.325
  208.4 4.8 slice.326
  261.4 24.3 %reduce-scatter.3.cloned.1.call-done = f32[2,8,8,256]{3,2,1,0:T(8,128)} async-done(((f32[64,8,8,256]{3,2,1,0:T(8,128)}), f32[2,8,8,256]{3,2,1,0:T(8,128)}) %reduce-scatter.3.cloned.1.call-update) | async-done | bytes 131088 | tf_op jit(solution)/shard_map/reduce_scatter | solution.py:88
  287.4 2.5 fusion.96
  290.7 8.8 slice.299
  299.5 8.8 slice.300
  308.3 7.0 slice.301
  315.3 7.1 slice.302
  322.4 7.1 slice.303
  329.5 7.1 slice.304
  336.5 7.4 slice.305
  344.0 7.4 slice.306
  351.4 7.4 slice.307
  358.8 7.4 slice.308
  366.2 7.4 slice.309
  373.7 7.4 slice.310
  381.1 7.4 slice.311
  388.5 7.4 slice.312
  396.0 7.4 slice.313
  419.2 240.9 %all-reduce.8.cloned.1.call-done = f32[3,3,3,128,256]{4,3,2,1,0:T(8,128)} async-done(((f32[3,3,3,128,256]{4,3,2,1,0:T(8,128)}), f32[3,3,3,128,256]{4,3,2,1,0:T(8,128)}) %all-reduce.8.cloned.1.call-update) | async-done | bytes 3538960
  661.7 244.3 %all-reduce.10.cloned.1.call-done = (f32[3,3,3,256,16]{3,4,2,1,0:T(8,128)}, f32[3,3,3,4,256]{4,3,2,1,0:T(4,128)}) async-done(((f32[3,3,3,256,16]{3,4,2,1,0:T(8,128)}, f32[3,3,3,4,256]{4,3,2,1,0:T(4,128)}), (f32[3,3,3,256,16]{3,4,2,1,0:T(8,128)}, f32[3,3,3,4,256]{4,3,2,1,0:T(4,128)})) %all-reduce.10.cloned.1.call-update) | async-done | bytes 552976 | tf_op jit(solution)/shard_map/psum | solution.py:106
  (136 shorter events, 102.2 us)
Async XLA Ops:
  7.2 278.6 %reduce-scatter.3.cloned.1.call-start = ((), (), s32[]{:S(2)}) async-start(), calls=%async_computation.1 | async-start | bytes 4325376 | tf_op jit(solution)/shard_map/reduce_scatter | solution.py:88
  34.8 5.4 copy-start
  34.8 625.2 %all-reduce.8.cloned.1.call-start = ((), (), s32[]{:S(2)}) async-start(), calls=%async_computation.2 | async-start | bytes 7077888
  36.5 118.5 %collective-permute-start = (bf16[1,1,16,16,128]{4,3,2,1,0:T(8,128)(2,1)}, bf16[1,1,16,16,128]{4,3,2,1,0:T(8,128)(2,1)}, u32[]{:S(2)}, u32[]{:S(2)}) collective-permute-start(bf16[1,1,16,16,128]{4,3,2,1,0:T(8,128)(2,1)} %slice.314), channel_id=1, source_target_pairs={{0,1},{1,2},{2,3},{3,4},{4,5},{5,6},{6,7},{7,8},{8,9},{9,10},{10,1... | collective-permute-start | bytes 196616 | tf_op jit(solution)/shard_map/ppermute | solution.py:12
  289.9 616.1 %all-reduce.10.cloned.1.call-start = ((), (), s32[]{:S(2)}) async-start(), calls=%async_computation.3 | async-start | bytes 1105920 | tf_op jit(solution)/shard_map/psum | solution.py:106
Sparse Core Ops, SparseCore 0:
  34.9 250.8 reduce-scatter.2
  290.0 369.9 all-reduce.7
  663.9 242.0 all-reduce.9
where the time goes:
time: 931 us; the launch traced here: 916 us
  waiting for transfers between devices  510 us (55%)
  local copies, waits for them, and re-layouts  341 us (37%)
  matrix products  41.1 us (4%)
  between operations  14.9 us (2%)
    psum x1, waiting for transfers between devices, body(): total_upper, total_lower = lax.psum((grad_upper, lower_share), 'sample')  244 us
    unnamed x4, waiting for transfers between devices  241 us
    slice x27, local copies, waits for them, and re-layouts, body(): padded_64[depth_tap:depth_tap + 2 * depth:2, row_tap:row_tap + 2 * height...  208 us
    slice x27, local copies, waits for them, and re-layouts, tap_stack(): padded_grid[depth_tap:depth_tap + 2 * depth:2, row_tap:row_tap + 2 * heig...  63 us
    dot_general x27, matrix products, body(): jnp.einsum('zyxc,zyxf->cf', window, cot_local, preferred_element_type=jnp...  29.1 us
    another operation x28, local copies, waits for them, and re-layouts, tap_stack(): return jnp.stack(tap_list)  25.3 us
    reduce_scatter x1, waiting for transfers between devices, body(): lax.psum_scatter(partial_64, 'chan', scatter_dimension=0, tiled=True)  24.3 us
    unnamed x40, local copies, waits for them, and re-layouts  22.9 us
  transfers between devices with their start and end apart: 4, of which 3 were waited for; matrix products, arithmetic and copies ran while one was open for 38% of the time, Pallas kernels for 0%

commit v1 on v0

v1 whole, which is shorter than its diff:
```python
import jax
import jax.numpy as jnp
import numpy as np
from jax import lax
from jax.experimental import pallas as pl
from jax.experimental.pallas import tpu as pltpu
from jax.sharding import PartitionSpec as P

leak_slope = 0.3
BF = jnp.bfloat16
F32 = jnp.float32
NX, NZL, NC = 4, 3, 2
NZH, NY = 4, 8
NM = NX * NC
NZ = NZH * NZL
PIECE = 56


def tap_of(par, shift):
    if par == 0:
        return 1 if shift == 0 else None
    return 2 if shift == 0 else 0


def class_taps(p):
    found = []
    for q in range(8):
        taps = [tap_of((p >> b) & 1, (q >> b) & 1) for b in (2, 1, 0)]
        if None not in taps:
            found.append((q, taps[0] * 9 + taps[1] * 3 + taps[2]))
    return found


def tables():
    split = np.zeros((256, 256), np.float32)
    for p in range(8):
        pz, py, px = p >> 2, (p >> 1) & 1, p & 1
        for a in range(2):
            for b in range(4):
                for c in range(4):
                    split[p * 32 + a * 16 + b * 4 + c, (2 * a + pz) * 64 + (2 * b + py) * 8 + 2 * c + px] = 1
    merge = np.zeros((128, 128), np.float32)
    for p in range(8):
        pz, py, px = p >> 2, (p >> 1) & 1, p & 1
        for b in range(4):
            for c in range(4):
                merge[pz * 64 + (2 * b + py) * 8 + 2 * c + px, p * 16 + b * 4 + c] = 1
    spread16 = np.zeros((16, 128), np.float32)
    for q in range(8):
        for f in range(16):
            spread16[f, q * 16 + f] = 1
    shift = np.zeros((128, 512), np.float32)
    for k in range(4):
        dy, dx = k >> 1, k & 1
        for a in range(8):
            for b in range(4 - dy):
                for c in range(4 - dx):
                    shift[a * 16 + b * 4 + c, k * 128 + a * 16 + (b + dy) * 4 + c + dx] = 1
    order = np.zeros((128, 128), np.float32)
    for m in range(NM):
        for h in range(2):
            for y in range(8):
                order[m * 16 + h * 8 + y, 4 * ((2 * (m % 2) + h) * 8 + y) + m // 2] = 1
    pick = np.zeros((9, 512, 128), np.float32)
    for j in range(3):
        for k in range(3):
            for z in range(2):
                for y in range(8):
                    for x in range(8):
                        row, col = 2 * y + j - 1, 2 * x + k - 1
                        if row >= 0 and col >= 0:
                            pick[j * 3 + k, z * 256 + row * 16 + col, z * 64 + y * 8 + x] = 1
    return split, merge, spread16, shift, order, pick


def mm(a, b):
    return jnp.dot(a, b, preferred_element_type=F32)


def kernel(
    act_ref, cot_ref, filt_ref, low_ref,
    split_ref, merge_ref, spread_ref, shift_ref, order_ref, pick_ref,
    out_up, out_low, out_cot,
    w_ref, wq_ref, a_ref, u_ref, urecv, uzl, ufin,
    fm1, fp1, fp2, r_ref, part, rplus, rminus,
    rim, t_ref, lstack, lsend, lrecv, cown, crecv, res,
    dsend, drecv, ssum, zsend, zrecv, xrecv,
    send_sem, recv_sem,
):
    s = lax.axis_index("sample")
    ch = lax.axis_index("chan")
    c = s % 2
    zl = (s // 2) % 3
    x = s // 6
    y = ch % 8
    zh = ch // 8
    m = x * 2 + c

    def at_zh(d):
        return (s, lax.rem(zh + d, NZH) * 8 + y)

    def at_y(d):
        return (s, zh * 8 + lax.rem(y + d, NY))

    def m_at(r):
        return lax.rem(m + r, NM)

    def at_m(r):
        mm_ = m_at(r)
        return (((mm_ // 2) * 3 + zl) * 2 + mm_ % 2, ch)

    def at_z(zl_, zh_):
        return ((x * 3 + zl_) * 2 + c, zh_ * 8 + y)

    counter = [0]
    pending = []

    def remote(src, dst, dev):
        i = counter[0]
        counter[0] += 1
        cp = pltpu.make_async_remote_copy(
            src_ref=src, dst_ref=dst, send_sem=send_sem.at[i], recv_sem=recv_sem.at[i],
            device_id=dev, device_id_type=pl.DeviceIdType.MESH,
        )
        cp.start()
        pending.append(cp)
        return cp

    barrier = pltpu.get_barrier_semaphore()
    partners = [at_y(d) for d in range(1, 8)] + [at_m(r) for r in range(1, 8)]
    partners += [(s, lax.rem(ch + 1, 32)), (s, lax.rem(ch + 31, 32))]
    for dzl in range(3):
        for dzh in range(4):
            if dzl or dzh:
                partners.append(at_z(lax.rem(zl + dzl, 3), lax.rem(zh + dzh, 4)))
    for dev in partners:
        pl.semaphore_signal(barrier, inc=1, device_id=dev, device_id_type=pl.DeviceIdType.MESH)
    pl.semaphore_wait(barrier, len(partners))

    h0 = 13 * c
    lo, hi = pl.ds(h0, 7), pl.ds(h0 + 7, 7)
    f_p_lo = remote(filt_ref.at[lo], fm1.at[lo], at_zh(1))
    f_m_hi = remote(filt_ref.at[hi], fp1.at[hi], at_zh(3))
    f_p_hi = remote(filt_ref.at[hi], fm1.at[hi], at_zh(1))
    f_m_lo = remote(filt_ref.at[lo], fp1.at[lo], at_zh(3))
    rim_cp = remote(low_ref.at[3], rim, (s, lax.rem(ch + 1, 32)))

    wide = mm(cot_ref[...], spread_ref[...])
    lane = lax.broadcasted_iota(jnp.int32, (128, 128), 1) // 16
    for g in range(4):
        near = wide[128 * g : 128 * g + 128]
        far = wide[128 * g + 16 : 128 * g + 144]
        both = jnp.where(lane >= 4, far, near)
        terms = [jnp.where(lane % 4 == k, both, 0.0).astype(BF) for k in range(4)]
        w_ref[g] = mm(shift_ref[...], jnp.concatenate(terms, axis=0)).astype(BF)
    w_cps = []
    for d in range(1, 4):
        w_cps.append(remote(w_ref.at[lax.rem(zh + d, NZH)], wq_ref.at[4 - d], at_zh(d)))

    def split_group(g, carry):
        got = mm(split_ref[...], act_ref[pl.ds(pl.multiple_of(g * 256, 256), 256), :]).astype(BF)
        for p in range(8):
            a_ref[p, pl.ds(pl.multiple_of(g * 32, 32), 32), :] = got[p * 32 : p * 32 + 32]
        return carry

    lax.fori_loop(0, 16, split_group, 0)

    f_p_lo.wait_recv()
    f2_p = remote(fm1.at[lo], fp2.at[lo], at_zh(1))
    f_m_hi.wait_recv()
    f2_m = remote(fp1.at[hi], fp2.at[hi], at_zh(3))

    wt = jnp.concatenate([jnp.transpose(w_ref[g].astype(F32)) for g in range(4)], axis=1).astype(BF)
    for p in range(8):
        got = mm(wt, a_ref[p])
        for q, tap in class_taps(p):
            u_ref[tap * 16 : tap * 16 + 16, :] = got[q * 16 : q * 16 + 16]
    u_ref[432:448, :] = jnp.zeros((16, 256), F32)
    u_cps = []
    for r in range(1, NM):
        u_cps.append(remote(u_ref.at[pl.ds(m_at(r) * PIECE, PIECE)], urecv.at[r - 1], at_m(r)))

    mate = (s + 1 - 2 * c, ch)
    own_half = pl.ds(14 * c, 13)
    f_p_hi.wait_recv()
    ex1 = remote(fm1.at[own_half], fm1.at[own_half], mate)
    f_m_lo.wait_recv()
    ex2 = remote(fp1.at[own_half], fp1.at[own_half], mate)

    rim_cp.wait_recv()
    edge = rim[...]
    edge = jnp.where(ch == 0, jnp.zeros_like(edge), edge)
    for q in range(5):
        plane = edge if q == 0 else low_ref[q - 1]
        got = lax.dot_general(order_ref[...], plane, (((1,), (1,)), ((), ())), preferred_element_type=F32)
        t_ref[q] = got.astype(BF)
    for i in range(3):
        lstack[i * 128 : i * 128 + 128, 0:256] = t_ref[i]
        lstack[i * 128 : i * 128 + 128, 256:512] = t_ref[i + 2]

    def window(jk, carry):
        got = mm(lstack[...], pick_ref[jk]).astype(BF)
        for i in range(3):
            for k in range(NM):
                lsend[k, i * 9 + jk] = got[i * 128 + k * 16 : i * 128 + k * 16 + 16]
        return carry

    lax.fori_loop(0, 9, window, 0)
    l_cps = []
    for r in range(1, NM):
        l_cps.append(remote(lsend.at[m_at(r)], lrecv.at[r - 1], at_m(r)))

    f2_p.wait_recv()
    f2_m.wait_recv()
    ex3 = remote(fp2.at[own_half], fp2.at[own_half], mate)
    for cp in w_cps:
        cp.wait_recv()
    wq_ref[0] = w_ref[zh]
    for cp in (ex1, ex2, ex3):
        cp.wait_recv()

    shards = (filt_ref, fp1, fp2, fm1)
    left = jnp.concatenate([wq_ref[r] for r in range(4)], axis=1)
    for p in range(8):
        taps = dict(class_taps(p))
        for r in range(4):
            for q in range(8):
                row = r * 128 + q * 16
                if q in taps:
                    r_ref[row : row + 16, :] = shards[r][taps[q]]
                else:
                    r_ref[row : row + 16, :] = jnp.zeros((16, 256), BF)
        got = mm(left, r_ref[...])
        for k in range(8):
            part[k, p] = got[k * 16 : k * 16 + 16]

    halves = (pl.ds(0, 4), pl.ds(4, 4))
    plus = [[None] * 2 for _ in range(4)]
    minus = [[None] * 2 for _ in range(3)]
    for t in range(4):
        for h in range(2):
            o = lax.rem(y + 4 - t, NY)
            if t:
                plus[t - 1][h].wait_recv()
                part[o, halves[h]] = part[o, halves[h]] + rplus[t - 1, halves[h]]
            plus[t][h] = remote(part.at[o, halves[h]], rplus.at[t, halves[h]], at_y(1))
            if t < 3:
                o = lax.rem(y + 5 + t, NY)
                if t:
                    minus[t - 1][h].wait_recv()
                    part[o, halves[h]] = part[o, halves[h]] + rminus[t - 1, halves[h]]
                minus[t][h] = remote(part.at[o, halves[h]], rminus.at[t, halves[h]], at_y(7))
        if t == 1:
            piece = u_ref[pl.ds(pl.multiple_of(m * PIECE, 8), PIECE), :]
            for r in range(1, NM):
                u_cps[r - 1].wait_recv()
                piece = piece + urecv[r - 1]
            uzl[zl] = piece
            uz_cps = []
            for d in (1, 2):
                uz_cps.append(remote(uzl.at[zl], uzl.at[zl], at_z(lax.rem(zl + d, 3), zh)))
        if t == 3:
            for cp in uz_cps:
                cp.wait_recv()
            ufin[m] = (uzl[0] + uzl[1] + uzl[2]) * (1.0 / 24.0)
    for h in range(2):
        minus[2][h].wait_recv()
        plus[3][h].wait_recv()
    total = part[y] + rplus[3] + rminus[2]
    total = total.reshape(128, 256)
    natural = jnp.dot(merge_ref[...], total, preferred_element_type=F32, precision=lax.Precision.HIGHEST)
    own = act_ref[pl.ds(pl.multiple_of(ch * 128, 128), 128), :].astype(F32)
    cot = natural * jnp.where(own > 0, 1.0, leak_slope)
    out_cot[...] = cot
    cown[...] = cot.astype(BF)
    c_cps = []
    for r in range(1, NM):
        c_cps.append(remote(cown, crecv.at[r - 1], at_m(r)))
    ug_cps = []
    for r in range(1, NM):
        ug_cps.append(remote(ufin.at[m], ufin.at[m], at_m(r)))

    acc = mm(lsend[m].reshape(432, 128), cown[...])
    for r in range(1, NM):
        l_cps[r - 1].wait_recv()
        c_cps[r - 1].wait_recv()
        acc = acc + mm(lrecv[r - 1].reshape(432, 128), crecv[r - 1])
    for half in range(2):
        res[half] = acc[:, 128 * half : 128 * half + 128]
    for k in range(NY):
        for half in range(2):
            got = res[half, pl.ds(k, 54, stride=8), :].astype(BF)
            got = jnp.concatenate([got, jnp.zeros((10, 128), BF)], axis=0)
            dsend[k, :, 128 * half : 128 * half + 128] = got
    d_cps = []
    for r in range(1, NY):
        d_cps.append(remote(dsend.at[lax.rem(y + r, NY)], drecv.at[r - 1], at_y(r)))
    total = [res[half, pl.ds(y, 54, stride=8), :] for half in range(2)]
    for r in range(1, NY):
        d_cps[r - 1].wait_recv()
        for half in range(2):
            total[half] = total[half] + drecv[r - 1, 0:54, 128 * half : 128 * half + 128].astype(F32)
    for half in range(2):
        ssum[half] = total[half]
    for h in range(2):
        for half in range(2):
            got = ssum[half, pl.ds(h, 27, stride=2), :]
            zsend[h, :, 128 * half : 128 * half + 128] = jnp.concatenate([got, jnp.zeros((5, 128), F32)], axis=0)

    myz = zh * 3 + zl
    base = counter[0]
    counter[0] += NZ
    sends = []
    for h in range(2):
        for l in range(3):
            tz = 2 * c + h
            i = counter[0]
            counter[0] += 1
            away = jnp.logical_or(tz != zh, zl != l)
            cp = pltpu.make_async_remote_copy(
                src_ref=zsend.at[h], dst_ref=zrecv.at[myz], send_sem=send_sem.at[i],
                recv_sem=recv_sem.at[base + myz], device_id=at_z(l, tz),
                device_id_type=pl.DeviceIdType.MESH,
            )
            pl.when(away)(cp.start)
            sends.append((away, cp))
    home = zh // 2 == c

    @pl.when(home)
    def _():
        zrecv[myz] = zsend[zh - 2 * c]

    for j in range(NZ):
        cp = pltpu.make_async_remote_copy(
            src_ref=zsend.at[0], dst_ref=zrecv.at[j], send_sem=send_sem.at[base + j],
            recv_sem=recv_sem.at[base + j], device_id=at_z(zl, zh),
            device_id_type=pl.DeviceIdType.MESH,
        )
        pl.when(jnp.logical_and(home, myz != j))(cp.wait_recv)

    base = counter[0]
    counter[0] += NX
    bsends = []

    @pl.when(home)
    def _():
        done = zrecv[0]
        for j in range(1, NZ):
            done = done + zrecv[j]
        xrecv[x] = done * (1.0 / 24.0)

    for r in range(1, NM):
        i = counter[0]
        counter[0] += 1
        cp = pltpu.make_async_remote_copy(
            src_ref=xrecv.at[x], dst_ref=xrecv.at[x], send_sem=send_sem.at[i],
            recv_sem=recv_sem.at[base + x], device_id=at_m(r),
            device_id_type=pl.DeviceIdType.MESH,
        )
        pl.when(home)(cp.start)
        bsends.append(cp)
    for cp in ug_cps:
        cp.wait_recv()
    for k in range(NM):
        out_up[k * PIECE : k * PIECE + PIECE, :] = ufin[k]
    for k in range(NX):
        cp = pltpu.make_async_remote_copy(
            src_ref=xrecv.at[k], dst_ref=xrecv.at[k], send_sem=send_sem.at[base + k],
            recv_sem=recv_sem.at[base + k], device_id=at_m(1),
            device_id_type=pl.DeviceIdType.MESH,
        )
        pl.when(jnp.logical_not(jnp.logical_and(home, x == k)))(cp.wait_recv)
    for k in range(NX):
        out_low[:, k, :] = xrecv[k, 0:27]

    for cp in pending:
        cp.wait_send()
    for away, cp in sends:
        pl.when(away)(cp.wait_send)
    for cp in bsends:
        pl.when(home)(cp.wait_send)


def body(act_64, cot_32, filters_32, act_128):
    consts = [jnp.asarray(t, BF) for t in tables()]
    consts[1] = consts[1].astype(F32)
    act = act_64.reshape(64 * 64, 256)
    cot = jnp.pad(cot_32[0].reshape(512, 16), ((0, 16), (0, 0)))
    filt = filters_32.transpose(0, 1, 2, 4, 3).reshape(27, 16, 256)
    low = act_128.reshape(4, 256, 128)
    vm = pltpu.VMEM
    up, lowg, cot_full = pl.pallas_call(
        kernel,
        out_shape=(
            jax.ShapeDtypeStruct((448, 256), F32),
            jax.ShapeDtypeStruct((27, 4, 256), F32),
            jax.ShapeDtypeStruct((128, 256), F32),
        ),
        in_specs=[pl.BlockSpec(memory_space=pltpu.VMEM)] * 10,
        out_specs=[pl.BlockSpec(memory_space=pltpu.VMEM)] * 3,
        scratch_shapes=[
            vm((4, 128, 128), BF), vm((4, 128, 128), BF), vm((8, 512, 256), BF),
            vm((448, 256), F32), vm((7, PIECE, 256), F32), vm((3, PIECE, 256), F32), vm((NM, PIECE, 256), F32),
            vm((27, 16, 256), BF), vm((27, 16, 256), BF), vm((27, 16, 256), BF),
            vm((512, 256), BF), vm((8, 8, 16, 256), F32), vm((4, 8, 16, 256), F32), vm((3, 8, 16, 256), F32),
            vm((256, 128), BF), vm((5, 128, 256), BF), vm((384, 512), BF),
            vm((NM, 27, 16, 128), BF), vm((7, 27, 16, 128), BF),
            vm((128, 256), BF), vm((7, 128, 256), BF), vm((2, 432, 128), F32),
            vm((8, 64, 256), BF), vm((7, 64, 256), BF), vm((2, 54, 128), F32),
            vm((2, 32, 256), F32), vm((NZ, 32, 256), F32), vm((NX, 32, 256), F32),
            pltpu.SemaphoreType.DMA((112,)), pltpu.SemaphoreType.DMA((112,)),
        ],
        compiler_params=pltpu.CompilerParams(
            collective_id=0, has_side_effects=True, vmem_limit_bytes=48 * 1024 * 1024
        ),
    )(act, cot, filt, low, *consts)
    up = up[:432].reshape(3, 3, 3, 16, 256).transpose(0, 1, 2, 4, 3)
    return up, lowg.reshape(3, 3, 3, 4, 256), cot_full.reshape(1, 2, 8, 8, 256)


def solution(mesh):
    placed = (
        P("sample", None, None, None, None),
        P("sample", None, None, None, "chan"),
        P(None, None, None, None, "chan"),
        P("sample", "chan", None, None, None),
    )
    return jax.shard_map(
        body,
        mesh=mesh,
        in_specs=placed,
        out_specs=(
            P(None, None, None, None, "chan"),
            P(None, None, None, "chan", None),
            P("sample", "chan", None, None, None),
        ),
        check_vma=False,
    )
```

time: 931 us -> 104 us (0.11)
  the two profiles are of different devices: /device:TPU:208 before, /device:TPU:1 now
where the time goes in v1:
time: 104 us
  Pallas kernels  91.3 us (88%)
  local copies, waits for them, and re-layouts  11.9 us (11%)
    pallas_call x1, Pallas kernels, body(): pl.pallas_call(kernel, out_shape=(jax.ShapeDtypeStruct((448, 256), F32),...  91.3 us
    unnamed x21, local copies, waits for them, and re-layouts  11.1 us

profile of v1, /device:TPU:1, one launch (start us, length us, event | category | flops | bytes accessed | tf_op | source)
XLA Modules:
  0.0 103.9 jit_solution(7491631834333892877)
XLA Ops:
  0.6 1.0 copy.13
  1.7 0.0 copy-start
  1.7 1.6 %copy-done = bf16[1,64,8,8,256]{4,3,2,1,0:T(8,128)(2,1)S(1)} copy-done((bf16[1,64,8,8,256]{4,3,2,1,0:T(8,128)(2,1)S(1)}, bf16[1,64,8,8,256]{4,3,2,1,0:T(8,128)(2,1)}, u32[]{:S(2)}) %copy-start) | copy-done | bytes 2097176
  3.3 0.0 copy-start.1
  3.3 1.3 %copy-done.1 = bf16[9,512,128]{2,1,0:T(8,128)(2,1)S(1)} copy-done((bf16[9,512,128]{2,1,0:T(8,128)(2,1)S(1)}, bf16[9,512,128]{2,1,0:T(8,128)(2,1)}, u32[]{:S(2)}) %copy-start.1) | copy-done | bytes 1179672
  4.5 0.0 copy-start.2
  4.5 0.9 copy-done.2
  5.5 0.0 copy-start.3
  5.5 0.9 copy-done.3
  6.4 0.0 copy-start.4
  6.4 0.9 copy-done.4
  7.3 0.0 copy-start.5
  7.3 0.9 copy-done.5
  8.2 0.0 copy-start.6
  8.2 0.8 copy-done.6
  9.1 0.0 copy-start.7
  9.1 0.8 copy-done.7
  9.8 0.0 copy-start.8
  9.8 0.7 copy-done.8
  10.5 91.3 %shard_map.121 = (f32[448,256]{1,0:T(8,128)S(1)}, f32[27,4,256]{2,1,0:T(4,128)S(1)}, f32[128,256]{1,0:T(8,128)S(1)}) custom-call(bf16[4096,256]{1,0:T(8,128)(2,1)S(1)} %bitcast.11, bf16[528,16]{1,0:T(8,128)(2,1)S(1)} %pad.4.cot_ref, bf16[27,16,256]{2,1,0:T(8,128)(2,1)S(1)} %bitcast.13, bf16[4,256,128]{2,1,0:T(8,128)(2,1)S(1)} %bitcast.12, ...), custom_call_target="tpu_custom_call" | custom-call | tf_op jit(solution)/shard_map/pallas_call | solution.py:392
  101.8 0.8 slice.3
  102.6 0.6 copy.16
  103.2 0.7 copy.17
  (1 shorter events, 0.0 us)
Async XLA Ops:
  1.7 1.6 %copy-start = (bf16[1,64,8,8,256]{4,3,2,1,0:T(8,128)(2,1)S(1)}, bf16[1,64,8,8,256]{4,3,2,1,0:T(8,128)(2,1)}, u32[]{:S(2)}) copy-start(bf16[1,64,8,8,256]{4,3,2,1,0:T(8,128)(2,1)} %param.10) | copy-start | bytes 6291460
  3.3 1.3 %copy-start.1 = (bf16[9,512,128]{2,1,0:T(8,128)(2,1)S(1)}, bf16[9,512,128]{2,1,0:T(8,128)(2,1)}, u32[]{:S(2)}) copy-start(bf16[9,512,128]{2,1,0:T(8,128)(2,1)} %constant.20.clone.pick_ref) | copy-start | bytes 3538948
  4.5 0.9 copy-start.2
  5.5 0.9 copy-start.3
  6.4 0.9 copy-start.4
  7.3 0.9 copy-start.5
  8.2 0.8 copy-start.6
  9.1 0.8 copy-start.7
  9.8 0.7 copy-start.8

commit v2 on v1

v2 whole, which is shorter than its diff:
```python
import jax
import jax.numpy as jnp
import numpy as np
from jax import lax
from jax.experimental import pallas as pl
from jax.experimental.pallas import tpu as pltpu
from jax.sharding import PartitionSpec as P

leak_slope = 0.3
BF = jnp.bfloat16
F32 = jnp.float32
NX, NZL, NC = 4, 3, 2
NZH, NY = 4, 8
NM = NX * NC
NZ = NZH * NZL
PIECE = 56


def tap_of(par, shift):
    if par == 0:
        return 1 if shift == 0 else None
    return 2 if shift == 0 else 0


def class_taps(p):
    found = []
    for q in range(8):
        taps = [tap_of((p >> b) & 1, (q >> b) & 1) for b in (2, 1, 0)]
        if None not in taps:
            found.append((q, taps[0] * 9 + taps[1] * 3 + taps[2]))
    return found


def tables():
    split = np.zeros((256, 256), np.float32)
    for p in range(8):
        pz, py, px = p >> 2, (p >> 1) & 1, p & 1
        for a in range(2):
            for b in range(4):
                for c in range(4):
                    split[p * 32 + a * 16 + b * 4 + c, (2 * a + pz) * 64 + (2 * b + py) * 8 + 2 * c + px] = 1
    merge = np.zeros((128, 128), np.float32)
    for p in range(8):
        pz, py, px = p >> 2, (p >> 1) & 1, p & 1
        for b in range(4):
            for c in range(4):
                merge[pz * 64 + (2 * b + py) * 8 + 2 * c + px, p * 16 + b * 4 + c] = 1
    spread16 = np.zeros((16, 128), np.float32)
    for q in range(8):
        for f in range(16):
            spread16[f, q * 16 + f] = 1
    shift = np.zeros((128, 512), np.float32)
    for k in range(4):
        dy, dx = k >> 1, k & 1
        for a in range(8):
            for b in range(4 - dy):
                for c in range(4 - dx):
                    shift[a * 16 + b * 4 + c, k * 128 + a * 16 + (b + dy) * 4 + c + dx] = 1
    order = np.zeros((128, 128), np.float32)
    for m in range(NM):
        for h in range(2):
            for y in range(8):
                order[m * 16 + h * 8 + y, 4 * ((2 * (m % 2) + h) * 8 + y) + m // 2] = 1
    pick = np.zeros((9, 512, 128), np.float32)
    for j in range(3):
        for k in range(3):
            for z in range(2):
                for y in range(8):
                    for x in range(8):
                        row, col = 2 * y + j - 1, 2 * x + k - 1
                        if row >= 0 and col >= 0:
                            pick[j * 3 + k, z * 256 + row * 16 + col, z * 64 + y * 8 + x] = 1
    return split, merge, spread16, shift, order, pick


def mm(a, b):
    return jnp.dot(a, b, preferred_element_type=F32)


def kernel(
    act_hbm, cot_hbm, filt_hbm, low_hbm,
    split_hbm, merge_hbm, spread_hbm, shift_hbm, order_hbm, pick_hbm,
    out_up, out_low, out_cot,
    act_ref, cot_ref, fbuf, low_ref,
    split_ref, merge_ref, spread_ref, shift_ref, order_ref, pick_ref,
    wide_ref, w_ref, wq_ref, a_ref, u_ref, urecv, uzl, ufin,
    r_ref, part, rlong, rshort,
    rim, t_ref, lstack, lsend, lrecv, call, res,
    dsend, drecv, ssum, zsend, zrecv, xrecv,
    load_sem, send_sem, recv_sem,
):
    s = lax.axis_index("sample")
    ch = lax.axis_index("chan")
    c = s % 2
    zl = (s // 2) % 3
    x = s // 6
    y = ch % 8
    zh = ch // 8
    m = x * 2 + c
    mate = (s + 1 - 2 * c, ch)

    def at_zh(d):
        return (s, lax.rem(zh + d, NZH) * 8 + y)

    def at_y(d):
        return (s, zh * 8 + lax.rem(y + d, NY))

    def m_at(r):
        return lax.rem(m + r, NM)

    def at_m(r):
        other = m_at(r)
        return (((other // 2) * 3 + zl) * 2 + other % 2, ch)

    def at_x(r):
        return ((lax.rem(x + r, NX) * 3 + zl) * 2 + c, ch)

    def from_x(r, core):
        return lax.rem(x + NX - r, NX) * 2 + core

    def at_z(zl_, zh_):
        return ((x * 3 + zl_) * 2 + c, zh_ * 8 + y)

    counter = [0]
    pending = []

    def remote(src, dst, dev):
        i = counter[0]
        counter[0] += 1
        cp = pltpu.make_async_remote_copy(
            src_ref=src, dst_ref=dst, send_sem=send_sem.at[i], recv_sem=recv_sem.at[i],
            device_id=dev, device_id_type=pl.DeviceIdType.MESH,
        )
        cp.start()
        pending.append(cp)
        return cp

    barrier = pltpu.get_barrier_semaphore()
    partners = [at_y(d) for d in range(1, 8)] + [at_m(r) for r in range(1, 8)]
    partners += [(s, lax.rem(ch + 1, 32)), (s, lax.rem(ch + 31, 32))]
    for dzl in range(3):
        for dzh in range(4):
            if dzl or dzh:
                partners.append(at_z(lax.rem(zl + dzl, 3), lax.rem(zh + dzh, 4)))
    for dev in partners:
        pl.semaphore_signal(barrier, inc=1, device_id=dev, device_id_type=pl.DeviceIdType.MESH)

    loads = {}
    for i, (name, src, dst) in enumerate((
        ("cot", cot_hbm, cot_ref), ("spread", spread_hbm, spread_ref), ("shift", shift_hbm, shift_ref),
        ("f0", filt_hbm.at[:, :, 0:128], fbuf.at[0, 0, 0:27]), ("f1", filt_hbm.at[:, :, 128:256], fbuf.at[0, 1, 0:27]),
        ("low", low_hbm, low_ref), ("split", split_hbm, split_ref), ("act", act_hbm, act_ref),
        ("order", order_hbm, order_ref), ("pick", pick_hbm, pick_ref), ("merge", merge_hbm, merge_ref),
    )):
        cp = pltpu.make_async_copy(src, dst, load_sem.at[i])
        cp.start()
        loads[name] = cp
    fbuf[0, :, 27] = jnp.zeros((2, 16, 128), BF)

    for name in ("cot", "spread", "shift"):
        loads[name].wait()
    for bc in range(16):
        got = lax.dot_general(
            cot_ref[bc * 16 : bc * 16 + 16, :], spread_ref[...], (((0,), (0,)), ((), ())), preferred_element_type=F32
        )
        wide_ref[pl.ds(bc, 32, stride=16), :] = got
    wide_ref[512:528, :] = jnp.zeros((16, 128), F32)
    lane = lax.broadcasted_iota(jnp.int32, (128, 128), 1) // 16
    for g in range(4):
        near = wide_ref[128 * g : 128 * g + 128, :]
        far = wide_ref[128 * g + 16 : 128 * g + 144, :]
        both = jnp.where(lane >= 4, far, near)
        terms = [jnp.where(lane % 4 == k, both, 0.0).astype(BF) for k in range(4)]
        w_ref[g] = mm(shift_ref[...], jnp.concatenate(terms, axis=0)).astype(BF)
    for name in ("f0", "f1", "low"):
        loads[name].wait()

    pl.semaphore_wait(barrier, len(partners))

    share = pl.ds(7 * x, 7)
    f_z = {}
    for d in (2, 1, 3):
        f_z[d] = remote(fbuf.at[0, c, share], fbuf.at[4 - d, c, share], at_zh(d))
    rim_cp = remote(low_ref.at[3], rim, (s, lax.rem(ch + 1, 32)))
    w_cps = []
    for d in (2, 1, 3):
        w_cps.append(remote(w_ref.at[lax.rem(zh + d, NZH)], wq_ref.at[4 - d], at_zh(d)))

    loads["split"].wait()
    loads["act"].wait()

    def split_group(g, carry):
        got = mm(split_ref[...], act_ref[pl.ds(pl.multiple_of(g * 256, 256), 256), :]).astype(BF)
        for p in range(8):
            a_ref[p, pl.ds(pl.multiple_of(g * 32, 32), 32), :] = got[p * 32 : p * 32 + 32]
        return carry

    lax.fori_loop(0, 16, split_group, 0)

    f_x = {}
    f_c = {}

    def spread_x(d):
        f_z[d].wait_recv()
        f_x[d] = [remote(fbuf.at[4 - d, c, share], fbuf.at[4 - d, c, share], at_x(r)) for r in (2, 1, 3)]

    def spread_c(d):
        for cp in f_x[d]:
            cp.wait_recv()
        f_c[d] = remote(fbuf.at[4 - d, c], fbuf.at[4 - d, c], mate)

    spread_x(1)
    spread_x(3)

    wt = jnp.concatenate([jnp.transpose(w_ref[g].astype(F32)) for g in range(4)], axis=1).astype(BF)
    for p in range(8):
        got = mm(wt, a_ref[p])
        for q, tap in class_taps(p):
            u_ref[tap * 16 : tap * 16 + 16, :] = got[q * 16 : q * 16 + 16]
    u_ref[432:448, :] = jnp.zeros((16, 256), F32)
    spread_x(2)
    spread_c(1)
    spread_c(3)
    u_cps = []
    for r in range(1, NM):
        u_cps.append(remote(u_ref.at[pl.ds(m_at(r) * PIECE, PIECE)], urecv.at[r - 1], at_m(r)))

    loads["order"].wait()
    loads["pick"].wait()
    rim_cp.wait_recv()
    edge = rim[...]
    edge = jnp.where(ch == 0, jnp.zeros_like(edge), edge)
    for q in range(5):
        plane = edge if q == 0 else low_ref[q - 1]
        got = lax.dot_general(order_ref[...], plane, (((1,), (1,)), ((), ())), preferred_element_type=F32)
        t_ref[q] = got.astype(BF)
    for i in range(3):
        lstack[i * 128 : i * 128 + 128, 0:256] = t_ref[i]
        lstack[i * 128 : i * 128 + 128, 256:512] = t_ref[i + 2]
    spread_c(2)

    for cp in w_cps:
        cp.wait_recv()
    wq_ref[0] = w_ref[zh]
    left = jnp.concatenate([wq_ref[r] for r in range(4)], axis=1)
    for d in (1, 3, 2):
        f_c[d].wait_recv()

    def partial(p):
        taps = dict(class_taps(p))
        for r in range(4):
            for q in range(8):
                row = r * 128 + q * 16
                for half in range(2):
                    lanes = slice(128 * half, 128 * half + 128)
                    if q in taps:
                        r_ref[p % 2, row : row + 16, lanes] = fbuf[r, half, taps[q]]
                    else:
                        r_ref[p % 2, row : row + 16, lanes] = jnp.zeros((16, 128), BF)
        got = mm(left, r_ref[p % 2])
        for k in range(8):
            part[k, p] = got[k * 16 : k * 16 + 16]

    halves = (pl.ds(0, 4), pl.ds(4, 4))
    way = (1, 7)
    back = (7, 1)
    longs = [[None] * 2 for _ in range(4)]
    shorts = [[None] * 2 for _ in range(3)]

    def ring(t, h):
        o = lax.rem(y + way[h] * (4 - t), NY)
        if t:
            longs[t - 1][h].wait_recv()
            part[o, halves[h]] = part[o, halves[h]] + rlong[t - 1, halves[h]]
        longs[t][h] = remote(part.at[o, halves[h]], rlong.at[t, halves[h]], at_y(way[h]))
        if t < 3:
            o = lax.rem(y + back[h] * (3 - t), NY)
            if t:
                shorts[t - 1][h].wait_recv()
                part[o, halves[h]] = part[o, halves[h]] + rshort[t - 1, halves[h]]
            shorts[t][h] = remote(part.at[o, halves[h]], rshort.at[t, halves[h]], at_y(back[h]))

    for p in range(4):
        partial(p)
    ring(0, 0)
    for p in range(4, 8):
        partial(p)
    ring(0, 1)

    def window(jk, carry):
        got = mm(lstack[...], pick_ref[jk]).astype(BF)
        for i in range(3):
            for k in range(NM):
                lsend[k, i * 9 + jk] = got[i * 128 + k * 16 : i * 128 + k * 16 + 16]
        return carry

    lax.fori_loop(0, 3, window, 0)
    ring(1, 0)
    ring(1, 1)
    lax.fori_loop(3, 9, window, 0)
    l_cps = []
    for r in range(1, NM):
        l_cps.append(remote(lsend.at[m_at(r)], lrecv.at[m], at_m(r)))
    ring(2, 0)
    ring(2, 1)
    piece = u_ref[pl.ds(pl.multiple_of(m * PIECE, 8), PIECE), :]
    for r in range(1, NM):
        u_cps[r - 1].wait_recv()
        piece = piece + urecv[r - 1]
    uzl[zl] = piece
    uz_cps = []
    for d in (1, 2):
        uz_cps.append(remote(uzl.at[zl], uzl.at[zl], at_z(lax.rem(zl + d, 3), zh)))
    ring(3, 0)
    ring(3, 1)

    loads["merge"].wait()
    c_x = [[None] * 4 for _ in range(2)]
    c_m = [None] * 2
    for h in range(2):
        shorts[2][h].wait_recv()
        longs[3][h].wait_recv()
        total = part[y, halves[h]] + rlong[3, halves[h]] + rshort[2, halves[h]]
        total = total.reshape(64, 256)
        natural = jnp.dot(merge_ref[...], total, preferred_element_type=F32, precision=lax.Precision.HIGHEST)
        own = act_ref[pl.ds(pl.multiple_of(ch * 128 + h * 64, 64), 64), :].astype(F32)
        cot = natural * jnp.where(own > 0, 1.0, leak_slope)
        out_cot[h * 64 : h * 64 + 64, :] = cot
        call[m, h] = cot.astype(BF)
        for r in (2, 1, 3):
            c_x[h][r] = remote(call.at[m, h], call.at[m, h], at_x(r))
        c_m[h] = remote(call.at[m, h], call.at[m, h], mate)

    def term(lhs, src):
        rhs = jnp.concatenate([call[src, 0], call[src, 1]], axis=0)
        return mm(lhs.reshape(432, 128), rhs)

    acc = term(lsend[m], m)
    for cp in l_cps:
        cp.wait_recv()
    c_f = [[None] * 4 for _ in range(2)]
    for h in range(2):
        for r in (1, 3, 2):
            c_x[h][r].wait_recv()
            got = from_x(r, c)
            c_f[h][r] = remote(call.at[got, h], call.at[got, h], mate)
    for h in range(2):
        c_m[h].wait_recv()
    acc = acc + term(lrecv[x * 2 + 1 - c], x * 2 + 1 - c)
    for r in (1, 3, 2):
        acc = acc + term(lrecv[from_x(r, c)], from_x(r, c))
    for cp in uz_cps:
        cp.wait_recv()
    ufin[m] = (uzl[0] + uzl[1] + uzl[2]) * (1.0 / 24.0)
    for r in (1, 3, 2):
        for h in range(2):
            c_f[h][r].wait_recv()
        acc = acc + term(lrecv[from_x(r, 1 - c)], from_x(r, 1 - c))
    for half in range(2):
        res[half] = acc[:, 128 * half : 128 * half + 128]

    d_cps = [[None] * NY for _ in range(2)]
    for half in range(2):
        for k in range(NY):
            got = res[half, pl.ds(k, 54, stride=8), :].astype(BF)
            dsend[half, k] = jnp.concatenate([got, jnp.zeros((10, 128), BF)], axis=0)
        for r in (4, 3, 5, 2, 6, 1, 7):
            d_cps[half][r] = remote(dsend.at[half, lax.rem(y + r, NY)], drecv.at[half, r - 1], at_y(r))
    ug_cps = []
    for r in range(1, NM):
        ug_cps.append(remote(ufin.at[m], ufin.at[m], at_m(r)))

    myz = zh * 3 + zl
    home = zh // 2 == c
    zbase = counter[0]
    counter[0] += 2 * NZ
    zsends = []
    for half in range(2):
        total = res[half, pl.ds(y, 54, stride=8), :]
        for r in (1, 7, 2, 6, 3, 5, 4):
            d_cps[half][r].wait_recv()
            total = total + drecv[half, r - 1, 0:54].astype(F32)
        ssum[half] = total
        for h in range(2):
            got = ssum[half, pl.ds(h, 27, stride=2), :]
            zsend[half, h] = jnp.concatenate([got, jnp.zeros((5, 128), F32)], axis=0).astype(BF)
        for h in range(2):
            for l in range(3):
                tz = 2 * c + h
                i = counter[0]
                counter[0] += 1
                away = jnp.logical_or(tz != zh, zl != l)
                cp = pltpu.make_async_remote_copy(
                    src_ref=zsend.at[half, h], dst_ref=zrecv.at[half, myz], send_sem=send_sem.at[i],
                    recv_sem=recv_sem.at[zbase + half * NZ + myz], device_id=at_z(l, tz),
                    device_id_type=pl.DeviceIdType.MESH,
                )
                pl.when(away)(cp.start)
                zsends.append((away, cp))

    for cp in ug_cps:
        cp.wait_recv()
    for k in range(NM):
        rows = min(PIECE, 432 - k * PIECE)
        out_up[k * PIECE : k * PIECE + rows, :] = ufin[k, 0:rows]

    xbase = counter[0]
    counter[0] += 2 * NX
    xsends = []
    for half in range(2):

        @pl.when(home)
        def _():
            zrecv[half, myz] = zsend[half, zh - 2 * c]

        for j in range(NZ):
            cp = pltpu.make_async_remote_copy(
                src_ref=zsend.at[half, 0], dst_ref=zrecv.at[half, j], send_sem=send_sem.at[zbase + half * NZ + j],
                recv_sem=recv_sem.at[zbase + half * NZ + j], device_id=at_z(zl, zh),
                device_id_type=pl.DeviceIdType.MESH,
            )
            pl.when(jnp.logical_and(home, myz != j))(cp.wait_recv)

        @pl.when(home)
        def _():
            done = zrecv[half, 0].astype(F32)
            for j in range(1, NZ):
                done = done + zrecv[half, j].astype(F32)
            xrecv[half, x] = done * (1.0 / 24.0)

        for r in range(1, NM):
            i = counter[0]
            counter[0] += 1
            cp = pltpu.make_async_remote_copy(
                src_ref=xrecv.at[half, x], dst_ref=xrecv.at[half, x], send_sem=send_sem.at[i],
                recv_sem=recv_sem.at[xbase + half * NX + x], device_id=at_m(r),
                device_id_type=pl.DeviceIdType.MESH,
            )
            pl.when(home)(cp.start)
            xsends.append(cp)
    for half in range(2):
        for k in range(NX):
            cp = pltpu.make_async_remote_copy(
                src_ref=xrecv.at[half, k], dst_ref=xrecv.at[half, k], send_sem=send_sem.at[xbase + half * NX + k],
                recv_sem=recv_sem.at[xbase + half * NX + k], device_id=mate,
                device_id_type=pl.DeviceIdType.MESH,
            )
            pl.when(jnp.logical_not(jnp.logical_and(home, x == k)))(cp.wait_recv)
        for k in range(NX):
            out_low[:, k, 128 * half : 128 * half + 128] = xrecv[half, k, 0:27]

    for cp in pending:
        cp.wait_send()
    for away, cp in zsends:
        pl.when(away)(cp.wait_send)
    for cp in xsends:
        pl.when(home)(cp.wait_send)


def body(act_64, cot_32, filters_32, act_128):
    consts = [jnp.asarray(t, BF) for t in tables()]
    consts[1] = consts[1].astype(F32)[:64, :64]
    act = act_64.reshape(64 * 64, 256)
    cot = cot_32[0].transpose(1, 2, 3, 0).reshape(256, 32)
    filt = filters_32.transpose(0, 1, 2, 4, 3).reshape(27, 16, 256)
    low = act_128.reshape(4, 256, 128)
    operands = (act, cot, filt, low, *consts)
    vm = pltpu.VMEM
    up, lowg, cot_full = pl.pallas_call(
        kernel,
        out_shape=(
            jax.ShapeDtypeStruct((432, 256), F32),
            jax.ShapeDtypeStruct((27, 4, 256), F32),
            jax.ShapeDtypeStruct((128, 256), F32),
        ),
        in_specs=[pl.BlockSpec(memory_space=pltpu.HBM)] * 10,
        out_specs=[pl.BlockSpec(memory_space=pltpu.VMEM)] * 3,
        scratch_shapes=[
            vm(act.shape, BF), vm(cot.shape, BF), vm((4, 2, 28, 16, 128), BF), vm(low.shape, BF),
            *[vm(t.shape, t.dtype) for t in consts],
            vm((528, 128), F32), vm((4, 128, 128), BF), vm((4, 128, 128), BF), vm((8, 512, 256), BF),
            vm((448, 256), F32), vm((7, PIECE, 256), F32), vm((3, PIECE, 256), F32), vm((NM, PIECE, 256), F32),
            vm((2, 512, 256), BF), vm((8, 8, 16, 256), F32), vm((4, 8, 16, 256), F32), vm((3, 8, 16, 256), F32),
            vm((256, 128), BF), vm((5, 128, 256), BF), vm((384, 512), BF),
            vm((NM, 27, 16, 128), BF), vm((NM, 27, 16, 128), BF),
            vm((NM, 2, 64, 256), BF), vm((2, 432, 128), F32),
            vm((2, 8, 64, 128), BF), vm((2, 7, 64, 128), BF), vm((2, 54, 128), F32),
            vm((2, 2, 32, 128), BF), vm((2, NZ, 32, 128), BF), vm((2, NX, 32, 128), F32),
            pltpu.SemaphoreType.DMA((16,)), pltpu.SemaphoreType.DMA((192,)), pltpu.SemaphoreType.DMA((192,)),
        ],
        compiler_params=pltpu.CompilerParams(
            collective_id=0, has_side_effects=True, vmem_limit_bytes=67043328
        ),
    )(*operands)
    up = up.reshape(3, 3, 3, 16, 256).transpose(0, 1, 2, 4, 3)
    return up, lowg.reshape(3, 3, 3, 4, 256), cot_full.reshape(1, 2, 8, 8, 256)


def solution(mesh):
    placed = (
        P("sample", None, None, None, None),
        P("sample", None, None, None, "chan"),
        P(None, None, None, None, "chan"),
        P("sample", "chan", None, None, None),
    )
    return jax.shard_map(
        body,
        mesh=mesh,
        in_specs=placed,
        out_specs=(
            P(None, None, None, None, "chan"),
            P(None, None, None, "chan", None),
            P("sample", "chan", None, None, None),
        ),
        check_vma=False,
    )
```

time: 104 us -> 87.8 us (0.84)
  Pallas kernels: 91.3 us -> 82.1 us
  local copies, waits for them, and re-layouts: 11.9 us -> 4.92 us
    pallas_call x1, Pallas kernels: 91.3 us -> 82.1 us  [body(): pl.pallas_call(kernel, out_shape=(jax.ShapeDtypeStruct((432, 256), F32),...]
    unnamed x21 -> x3, local copies, waits for them, and re-layouts: 11.1 us -> 4.92 us
where the time goes in v2:
time: 87.8 us; the launch traced here: 87.6 us
  Pallas kernels  82.1 us (94%)
  local copies, waits for them, and re-layouts  4.92 us (6%)
    pallas_call x1, Pallas kernels, body(): pl.pallas_call(kernel, out_shape=(jax.ShapeDtypeStruct((432, 256), F32),...  82.1 us
    unnamed x3, local copies, waits for them, and re-layouts  4.92 us

profile of v2, /device:TPU:1, one launch (start us, length us, event | category | flops | bytes accessed | tf_op | source)
XLA Modules:
  0.0 87.6 jit_solution(6037631108683377145)
XLA Ops:
  0.6 82.1 %shard_map.121 = (f32[432,256]{1,0:T(8,128)}, f32[27,4,256]{2,1,0:T(4,128)}, f32[128,256]{1,0:T(8,128)}) custom-call(bf16[4096,256]{1,0:T(8,128)(2,1)} %bitcast.15, bf16[256,32]{1,0:T(8,128)(2,1)} %bitcast.21, bf16[27,16,256]{2,1,0:T(8,128)(2,1)} %bitcast.18, bf16[4,256,128]{2,1,0:T(8,128)(2,1)} %bitcast.17, bf16[256,256]{1,0:T(8,128)(2,1)} %constant.12.clone.split_hbm, ...), custom_call_target="tpu_custom_call" | custom-call | tf_op jit(solution)/shard_map/pallas_call | solution.py:469
  82.7 1.8 %copy.16 = f32[3,3,3,256,16]{3,4,2,1,0:T(8,128)} copy(f32[3,3,3,256,16]{3,4,2,1,0:T(8,128)} %bitcast.16) | data formatting | bytes 884736
  84.5 1.5 %copy.17 = f32[3,3,3,4,256]{4,3,2,1,0:T(4,128)} copy(f32[3,3,3,4,256]{4,3,2,1,0:T(4,128)} %bitcast.20) | data formatting | bytes 221184
  86.1 1.6 %copy.18 = f32[1,2,8,8,256]{4,3,2,1,0:T(8,128)} copy(f32[1,2,8,8,256]{4,3,2,1,0:T(8,128)} %bitcast.19) | data formatting | bytes 262144

commit v3 on v2

--- a/solution.py
+++ b/solution.py
@@ -70,7 +70,7 @@
                         row, col = 2 * y + j - 1, 2 * x + k - 1
                         if row >= 0 and col >= 0:
                             pick[j * 3 + k, z * 256 + row * 16 + col, z * 64 + y * 8 + x] = 1
-    return split, merge, spread16, shift, order, pick
+    return split, merge, spread16, shift, order, pick, np.eye(256, dtype=np.float32), np.tile(spread16, (16, 1))
 
 
 def mm(a, b):
@@ -79,11 +79,11 @@
 
 def kernel(
     act_hbm, cot_hbm, filt_hbm, low_hbm,
-    split_hbm, merge_hbm, spread_hbm, shift_hbm, order_hbm, pick_hbm,
+    split_hbm, merge_hbm, spread_hbm, shift_hbm, order_hbm, pick_hbm, eye_hbm, tall_hbm,
     out_up, out_low, out_cot,
     act_ref, cot_ref, fbuf, low_ref,
-    split_ref, merge_ref, spread_ref, shift_ref, order_ref, pick_ref,
-    wide_ref, w_ref, wq_ref, a_ref, u_ref, urecv, uzl, ufin,
+    split_ref, merge_ref, spread_ref, shift_ref, order_ref, pick_ref, eye_ref, tall_ref,
+    wide_ref, wide_far, planes, qsend, qrecv, w_ref, wq_ref, a_ref, u_ref, urecv, uzl, ufin,
     r_ref, part, rlong, rshort,
     rim, t_ref, lstack, lsend, lrecv, call, res,
     dsend, drecv, ssum, zsend, zrecv, xrecv,
@@ -147,9 +147,10 @@
 
     loads = {}
     for i, (name, src, dst) in enumerate((
-        ("cot", cot_hbm, cot_ref), ("spread", spread_hbm, spread_ref), ("shift", shift_hbm, shift_ref),
         ("f0", filt_hbm.at[:, :, 0:128], fbuf.at[0, 0, 0:27]), ("f1", filt_hbm.at[:, :, 128:256], fbuf.at[0, 1, 0:27]),
-        ("low", low_hbm, low_ref), ("split", split_hbm, split_ref), ("act", act_hbm, act_ref),
+        ("cot", cot_hbm, cot_ref), ("eye", eye_hbm, eye_ref), ("low", low_hbm, low_ref),
+        ("spread", spread_hbm, spread_ref), ("shift", shift_hbm, shift_ref), ("tall", tall_hbm, tall_ref),
+        ("split", split_hbm, split_ref), ("act", act_hbm, act_ref),
         ("order", order_hbm, order_ref), ("pick", pick_hbm, pick_ref), ("merge", merge_hbm, merge_ref),
     )):
         cp = pltpu.make_async_copy(src, dst, load_sem.at[i])
@@ -157,34 +158,45 @@
         loads[name] = cp
     fbuf[0, :, 27] = jnp.zeros((2, 16, 128), BF)
 
-    for name in ("cot", "spread", "shift"):
+    loads["cot"].wait()
+    loads["eye"].wait()
+    planes[0:32, :] = lax.dot_general(
+        cot_ref[...], eye_ref[...], (((0,), (0,)), ((), ())), preferred_element_type=F32
+    )
+    planes[32:40, :] = jnp.zeros((8, 256), F32)
+    for q in range(4):
+        qsend[q] = planes[8 * q : 8 * q + 16, :].astype(BF)
+    for name in ("f0", "f1", "low"):
         loads[name].wait()
+
+    pl.semaphore_wait(barrier, len(partners))
+
+    share = pl.ds(7 * x, 7)
+    f_z = {}
+    for d in (2, 1, 3):
+        f_z[d] = remote(fbuf.at[0, c, share], fbuf.at[4 - d, c, share], at_zh(d))
+    q_cps = []
+    for d in (2, 1, 3):
+        q_cps.append(remote(qsend.at[lax.rem(zh + d, NZH)], qrecv.at[3 - d], at_zh(d)))
+    rim_cp = remote(low_ref.at[3], rim, (s, lax.rem(ch + 1, 32)))
+
+    lane = lax.broadcasted_iota(jnp.int32, (128, 128), 1) // 16
+
+    def shifted(near, far):
+        both = jnp.where(lane >= 4, far, near)
+        terms = [jnp.where(lane % 4 == k, both, 0.0).astype(BF) for k in range(4)]
+        return mm(shift_ref[...], jnp.concatenate(terms, axis=0)).astype(BF)
+
+    loads["spread"].wait()
+    loads["shift"].wait()
     for bc in range(16):
         got = lax.dot_general(
             cot_ref[bc * 16 : bc * 16 + 16, :], spread_ref[...], (((0,), (0,)), ((), ())), preferred_element_type=F32
         )
         wide_ref[pl.ds(bc, 32, stride=16), :] = got
     wide_ref[512:528, :] = jnp.zeros((16, 128), F32)
-    lane = lax.broadcasted_iota(jnp.int32, (128, 128), 1) // 16
     for g in range(4):
-        near = wide_ref[128 * g : 128 * g + 128, :]
-        far = wide_ref[128 * g + 16 : 128 * g + 144, :]
-        both = jnp.where(lane >= 4, far, near)
-        terms = [jnp.where(lane % 4 == k, both, 0.0).astype(BF) for k in range(4)]
-        w_ref[g] = mm(shift_ref[...], jnp.concatenate(terms, axis=0)).astype(BF)
-    for name in ("f0", "f1", "low"):
-        loads[name].wait()
-
-    pl.semaphore_wait(barrier, len(partners))
-
-    share = pl.ds(7 * x, 7)
-    f_z = {}
-    for d in (2, 1, 3):
-        f_z[d] = remote(fbuf.at[0, c, share], fbuf.at[4 - d, c, share], at_zh(d))
-    rim_cp = remote(low_ref.at[3], rim, (s, lax.rem(ch + 1, 32)))
-    w_cps = []
-    for d in (2, 1, 3):
-        w_cps.append(remote(w_ref.at[lax.rem(zh + d, NZH)], wq_ref.at[4 - d], at_zh(d)))
+        w_ref[g] = shifted(wide_ref[128 * g : 128 * g + 128, :], wide_ref[128 * g + 16 : 128 * g + 144, :])
 
     loads["split"].wait()
     loads["act"].wait()
@@ -239,9 +251,18 @@
         lstack[i * 128 : i * 128 + 128, 256:512] = t_ref[i + 2]
     spread_c(2)
 
-    for cp in w_cps:
+    loads["tall"].wait()
+    for cp in q_cps:
         cp.wait_recv()
     wq_ref[0] = w_ref[zh]
+    group = lax.broadcasted_iota(jnp.int32, (48, 256), 1) // 16
+    rows = jnp.concatenate([qrecv[0], qrecv[1], qrecv[2]], axis=0).astype(F32)
+    for bc in range(16):
+        got = mm(jnp.where(group == bc, rows, 0.0).astype(BF), tall_ref[...])
+        for r in range(3):
+            wide_far[r, pl.ds(bc, 16, stride=16), :] = got[r * 16 : r * 16 + 16]
+    for r in range(3):
+        wq_ref[r + 1] = shifted(wide_far[r, 0:128, :], wide_far[r, 16:144, :])
     left = jnp.concatenate([wq_ref[r] for r in range(4)], axis=1)
     for d in (1, 3, 2):
         f_c[d].wait_recv()
@@ -457,6 +478,14 @@
         pl.when(home)(cp.wait_send)
 
 
+def flush(a, b, c, out_a, out_b, out_c, sem):
+    moves = [pltpu.make_async_copy(src, dst, sem.at[i]) for i, (src, dst) in enumerate(((a, out_a), (b, out_b), (c, out_c)))]
+    for cp in moves:
+        cp.start()
+    for cp in moves:
+        cp.wait()
+
+
 def body(act_64, cot_32, filters_32, act_128):
     consts = [jnp.asarray(t, BF) for t in tables()]
     consts[1] = consts[1].astype(F32)[:64, :64]
@@ -464,7 +493,7 @@
     cot = cot_32[0].transpose(1, 2, 3, 0).reshape(256, 32)
     filt = filters_32.transpose(0, 1, 2, 4, 3).reshape(27, 16, 256)
     low = act_128.reshape(4, 256, 128)
-    operands = (act, cot, filt, low, *consts)
+    operands = [pltpu.with_memory_space_constraint(t, pltpu.HBM) for t in (act, cot, filt, low, *consts)]
     vm = pltpu.VMEM
     up, lowg, cot_full = pl.pallas_call(
         kernel,
@@ -473,12 +502,13 @@
             jax.ShapeDtypeStruct((27, 4, 256), F32),
             jax.ShapeDtypeStruct((128, 256), F32),
         ),
-        in_specs=[pl.BlockSpec(memory_space=pltpu.HBM)] * 10,
+        in_specs=[pl.BlockSpec(memory_space=pltpu.HBM)] * len(operands),
         out_specs=[pl.BlockSpec(memory_space=pltpu.VMEM)] * 3,
         scratch_shapes=[
             vm(act.shape, BF), vm(cot.shape, BF), vm((4, 2, 28, 16, 128), BF), vm(low.shape, BF),
             *[vm(t.shape, t.dtype) for t in consts],
-            vm((528, 128), F32), vm((4, 128, 128), BF), vm((4, 128, 128), BF), vm((8, 512, 256), BF),
+            vm((528, 128), F32), vm((3, 256, 128), F32), vm((40, 256), F32), vm((4, 16, 256), BF), vm((3, 16, 256), BF),
+            vm((4, 128, 128), BF), vm((4, 128, 128), BF), vm((8, 512, 256), BF),
             vm((448, 256), F32), vm((7, PIECE, 256), F32), vm((3, PIECE, 256), F32), vm((NM, PIECE, 256), F32),
             vm((2, 512, 256), BF), vm((8, 8, 16, 256), F32), vm((4, 8, 16, 256), F32), vm((3, 8, 16, 256), F32),
             vm((256, 128), BF), vm((5, 128, 256), BF), vm((384, 512), BF),
@@ -489,9 +519,17 @@
             pltpu.SemaphoreType.DMA((16,)), pltpu.SemaphoreType.DMA((192,)), pltpu.SemaphoreType.DMA((192,)),
         ],
         compiler_params=pltpu.CompilerParams(
-            collective_id=0, has_side_effects=True, vmem_limit_bytes=67043328
+            collective_id=0, has_side_effects=True, vmem_limit_bytes=48 * 1024 * 1024
         ),
     )(*operands)
+    up, lowg, cot_full = pl.pallas_call(
+        flush,
+        out_shape=tuple(jax.ShapeDtypeStruct(t.shape, t.dtype) for t in (up, lowg, cot_full)),
+        in_specs=[pl.BlockSpec(memory_space=pltpu.VMEM)] * 3,
+        out_specs=[pl.BlockSpec(memory_space=pltpu.HBM)] * 3,
+        scratch_shapes=[pltpu.SemaphoreType.DMA((3,))],
+        compiler_params=pltpu.CompilerParams(vmem_limit_bytes=8 * 1024 * 1024),
+    )(up, lowg, cot_full)
     up = up.reshape(3, 3, 3, 16, 256).transpose(0, 1, 2, 4, 3)
     return up, lowg.reshape(3, 3, 3, 4, 256), cot_full.reshape(1, 2, 8, 8, 256)
 

time: 87.8 us -> 81.8 us (0.932)
  local copies, waits for them, and re-layouts: 4.92 us -> 0 us
  Pallas kernels: 82.1 us -> 81 us
    unnamed x3 -> x0, local copies, waits for them, and re-layouts: 4.92 us -> none
    pallas_call x1, Pallas kernels: 82.1 us -> 80.2 us  [body(): pl.pallas_call(kernel, out_shape=(jax.ShapeDtypeStruct((432, 256), F32),...]
where the time goes in v3:
time: 81.8 us; the launch traced here: 81.7 us
  Pallas kernels  81 us (99%)
    pallas_call x1, Pallas kernels, body(): pl.pallas_call(kernel, out_shape=(jax.ShapeDtypeStruct((432, 256), F32),...  80.2 us

profile of v3, /device:TPU:1, one launch (start us, length us, event | category | flops | bytes accessed | tf_op | source)
XLA Modules:
  0.0 81.7 jit_solution(15706131366524378919)
XLA Ops:
  0.6 80.2 %shard_map.139 = (f32[432,256]{1,0:T(8,128)S(1)}, f32[27,4,256]{2,1,0:T(4,128)S(1)}, f32[128,256]{1,0:T(8,128)S(1)}) custom-call(bf16[4096,256]{1,0:T(8,128)(2,1)} %bitcast.15, bf16[256,32]{1,0:T(8,128)(2,1)} %bitcast.18, bf16[27,16,256]{2,1,0:T(8,128)(2,1)} %bitcast.17, bf16[4,256,128]{2,1,0:T(8,128)(2,1)} %bitcast.16, ...), custom_call_target="tpu_custom_call" | custom-call | tf_op jit(solution)/shard_map/pallas_call | solution.py:498
  80.8 0.9 %shard_map.140 = (f32[432,256]{1,0:T(8,128)}, f32[27,4,256]{2,1,0:T(4,128)}, f32[128,256]{1,0:T(8,128)}) custom-call(f32[432,256]{1,0:T(8,128)S(1)} %get-tuple-element.9.a, f32[27,4,256]{2,1,0:T(4,128)S(1)} %get-tuple-element.10.b, f32[128,256]{1,0:T(8,128)S(1)} %get-tuple-element.11.c), custom_call_target="tpu_custom_call" | custom-call | tf_op jit(solution)/shard_map/pallas_call | solution.py:525

commit v4 on v3

--- a/solution.py
+++ b/solution.py
@@ -100,23 +100,23 @@
     mate = (s + 1 - 2 * c, ch)
 
     def at_zh(d):
-        return (s, lax.rem(zh + d, NZH) * 8 + y)
+        return (s, jnp.bitwise_and(zh + d, NZH - 1) * 8 + y)
 
     def at_y(d):
-        return (s, zh * 8 + lax.rem(y + d, NY))
+        return (s, zh * 8 + jnp.bitwise_and(y + d, NY - 1))
 
     def m_at(r):
-        return lax.rem(m + r, NM)
+        return jnp.bitwise_and(m + r, NM - 1)
 
     def at_m(r):
         other = m_at(r)
         return (((other // 2) * 3 + zl) * 2 + other % 2, ch)
 
     def at_x(r):
-        return ((lax.rem(x + r, NX) * 3 + zl) * 2 + c, ch)
+        return ((jnp.bitwise_and(x + r, NX - 1) * 3 + zl) * 2 + c, ch)
 
     def from_x(r, core):
-        return lax.rem(x + NX - r, NX) * 2 + core
+        return jnp.bitwise_and(x + NX - r, NX - 1) * 2 + core
 
     def at_z(zl_, zh_):
         return ((x * 3 + zl_) * 2 + c, zh_ * 8 + y)
@@ -141,7 +141,7 @@
     for dzl in range(3):
         for dzh in range(4):
             if dzl or dzh:
-                partners.append(at_z(lax.rem(zl + dzl, 3), lax.rem(zh + dzh, 4)))
+                partners.append(at_z(lax.rem(zl + dzl, 3), jnp.bitwise_and(zh + dzh, 3)))
     for dev in partners:
         pl.semaphore_signal(barrier, inc=1, device_id=dev, device_id_type=pl.DeviceIdType.MESH)
 
@@ -177,7 +177,7 @@
         f_z[d] = remote(fbuf.at[0, c, share], fbuf.at[4 - d, c, share], at_zh(d))
     q_cps = []
     for d in (2, 1, 3):
-        q_cps.append(remote(qsend.at[lax.rem(zh + d, NZH)], qrecv.at[3 - d], at_zh(d)))
+        q_cps.append(remote(qsend.at[jnp.bitwise_and(zh + d, NZH - 1)], qrecv.at[3 - d], at_zh(d)))
     rim_cp = remote(low_ref.at[3], rim, (s, lax.rem(ch + 1, 32)))
 
     lane = lax.broadcasted_iota(jnp.int32, (128, 128), 1) // 16
@@ -231,12 +231,6 @@
             u_ref[tap * 16 : tap * 16 + 16, :] = got[q * 16 : q * 16 + 16]
     u_ref[432:448, :] = jnp.zeros((16, 256), F32)
     spread_x(2)
-    spread_c(1)
-    spread_c(3)
-    u_cps = []
-    for r in range(1, NM):
-        u_cps.append(remote(u_ref.at[pl.ds(m_at(r) * PIECE, PIECE)], urecv.at[r - 1], at_m(r)))
-
     loads["order"].wait()
     loads["pick"].wait()
     rim_cp.wait_recv()
@@ -249,7 +243,25 @@
     for i in range(3):
         lstack[i * 128 : i * 128 + 128, 0:256] = t_ref[i]
         lstack[i * 128 : i * 128 + 128, 256:512] = t_ref[i + 2]
+    spread_c(1)
+    spread_c(3)
+
+    def window(jk, carry):
+        got = mm(lstack[...], pick_ref[jk]).astype(BF)
+        for i in range(3):
+            for k in range(NM):
+                lsend[k, i * 9 + jk] = got[i * 128 + k * 16 : i * 128 + k * 16 + 16]
+        return carry
+
+    lax.fori_loop(0, 9, window, 0)
     spread_c(2)
+    u_cps = []
+    for r in range(1, NM):
+        u_cps.append(remote(u_ref.at[pl.ds(m_at(r) * PIECE, PIECE)], urecv.at[r - 1], at_m(r)))
+
+    l_cps = []
+    for r in range(1, NM):
+        l_cps.append(remote(lsend.at[m_at(r)], lrecv.at[m], at_m(r)))
 
     loads["tall"].wait()
     for cp in q_cps:
@@ -282,48 +294,32 @@
         for k in range(8):
             part[k, p] = got[k * 16 : k * 16 + 16]
 
-    halves = (pl.ds(0, 4), pl.ds(4, 4))
-    way = (1, 7)
-    back = (7, 1)
-    longs = [[None] * 2 for _ in range(4)]
-    shorts = [[None] * 2 for _ in range(3)]
-
-    def ring(t, h):
-        o = lax.rem(y + way[h] * (4 - t), NY)
+    quarters = [pl.ds(2 * u, 2) for u in range(4)]
+    way = (1, 7, 1, 7)
+    back = (7, 1, 7, 1)
+    longs = [[None] * 4 for _ in range(4)]
+    shorts = [[None] * 4 for _ in range(3)]
+
+    def ring(t, u):
+        o = jnp.bitwise_and(y + way[u] * (4 - t), NY - 1)
         if t:
-            longs[t - 1][h].wait_recv()
-            part[o, halves[h]] = part[o, halves[h]] + rlong[t - 1, halves[h]]
-        longs[t][h] = remote(part.at[o, halves[h]], rlong.at[t, halves[h]], at_y(way[h]))
+            longs[t - 1][u].wait_recv()
+            part[o, quarters[u]] = part[o, quarters[u]] + rlong[t - 1, quarters[u]]
+        longs[t][u] = remote(part.at[o, quarters[u]], rlong.at[t, quarters[u]], at_y(way[u]))
         if t < 3:
-            o = lax.rem(y + back[h] * (3 - t), NY)
+            o = jnp.bitwise_and(y + back[u] * (3 - t), NY - 1)
             if t:
-                shorts[t - 1][h].wait_recv()
-                part[o, halves[h]] = part[o, halves[h]] + rshort[t - 1, halves[h]]
-            shorts[t][h] = remote(part.at[o, halves[h]], rshort.at[t, halves[h]], at_y(back[h]))
-
-    for p in range(4):
-        partial(p)
-    ring(0, 0)
-    for p in range(4, 8):
-        partial(p)
-    ring(0, 1)
-
-    def window(jk, carry):
-        got = mm(lstack[...], pick_ref[jk]).astype(BF)
-        for i in range(3):
-            for k in range(NM):
-                lsend[k, i * 9 + jk] = got[i * 128 + k * 16 : i * 128 + k * 16 + 16]
-        return carry
-
-    lax.fori_loop(0, 3, window, 0)
-    ring(1, 0)
-    ring(1, 1)
-    lax.fori_loop(3, 9, window, 0)
-    l_cps = []
-    for r in range(1, NM):
-        l_cps.append(remote(lsend.at[m_at(r)], lrecv.at[m], at_m(r)))
-    ring(2, 0)
-    ring(2, 1)
+                shorts[t - 1][u].wait_recv()
+                part[o, quarters[u]] = part[o, quarters[u]] + rshort[t - 1, quarters[u]]
+            shorts[t][u] = remote(part.at[o, quarters[u]], rshort.at[t, quarters[u]], at_y(back[u]))
+
+    for u in range(4):
+        partial(2 * u)
+        partial(2 * u + 1)
+        ring(0, u)
+    for t in (1, 2):
+        for u in range(4):
+            ring(t, u)
     piece = u_ref[pl.ds(pl.multiple_of(m * PIECE, 8), PIECE), :]
     for r in range(1, NM):
         u_cps[r - 1].wait_recv()
@@ -332,16 +328,18 @@
     uz_cps = []
     for d in (1, 2):
         uz_cps.append(remote(uzl.at[zl], uzl.at[zl], at_z(lax.rem(zl + d, 3), zh)))
-    ring(3, 0)
-    ring(3, 1)
+    for u in range(4):
+        ring(3, u)
 
     loads["merge"].wait()
     c_x = [[None] * 4 for _ in range(2)]
     c_m = [None] * 2
     for h in range(2):
-        shorts[2][h].wait_recv()
-        longs[3][h].wait_recv()
-        total = part[y, halves[h]] + rlong[3, halves[h]] + rshort[2, halves[h]]
+        for u in (2 * h, 2 * h + 1):
+            shorts[2][u].wait_recv()
+            longs[3][u].wait_recv()
+        both = pl.ds(4 * h, 4)
+        total = part[y, both] + rlong[3, both] + rshort[2, both]
         total = total.reshape(64, 256)
         natural = jnp.dot(merge_ref[...], total, preferred_element_type=F32, precision=lax.Precision.HIGHEST)
         own = act_ref[pl.ds(pl.multiple_of(ch * 128 + h * 64, 64), 64), :].astype(F32)
@@ -352,11 +350,16 @@
             c_x[h][r] = remote(call.at[m, h], call.at[m, h], at_x(r))
         c_m[h] = remote(call.at[m, h], call.at[m, h], mate)
 
-    def term(lhs, src):
-        rhs = jnp.concatenate([call[src, 0], call[src, 1]], axis=0)
-        return mm(lhs.reshape(432, 128), rhs)
-
-    acc = term(lsend[m], m)
+    def terms(core):
+        lhs = []
+        rhs = []
+        for r in range(NX):
+            src = from_x(r, core)
+            own = lsend[m] if r == 0 and core is c else lrecv[src]
+            lhs.append(own.reshape(432, 128))
+            rhs += [call[src, 0], call[src, 1]]
+        return mm(jnp.concatenate(lhs, axis=1), jnp.concatenate(rhs, axis=0))
+
     for cp in l_cps:
         cp.wait_recv()
     c_f = [[None] * 4 for _ in range(2)]
@@ -365,18 +368,16 @@
             c_x[h][r].wait_recv()
             got = from_x(r, c)
             c_f[h][r] = remote(call.at[got, h], call.at[got, h], mate)
-    for h in range(2):
-        c_m[h].wait_recv()
-    acc = acc + term(lrecv[x * 2 + 1 - c], x * 2 + 1 - c)
-    for r in (1, 3, 2):
-        acc = acc + term(lrecv[from_x(r, c)], from_x(r, c))
     for cp in uz_cps:
         cp.wait_recv()
     ufin[m] = (uzl[0] + uzl[1] + uzl[2]) * (1.0 / 24.0)
+    acc = terms(c)
+    for h in range(2):
+        c_m[h].wait_recv()
     for r in (1, 3, 2):
         for h in range(2):
             c_f[h][r].wait_recv()
-        acc = acc + term(lrecv[from_x(r, 1 - c)], from_x(r, 1 - c))
+    acc = acc + terms(1 - c)
     for half in range(2):
         res[half] = acc[:, 128 * half : 128 * half + 128]
 
@@ -386,7 +387,7 @@
             got = res[half, pl.ds(k, 54, stride=8), :].astype(BF)
             dsend[half, k] = jnp.concatenate([got, jnp.zeros((10, 128), BF)], axis=0)
         for r in (4, 3, 5, 2, 6, 1, 7):
-            d_cps[half][r] = remote(dsend.at[half, lax.rem(y + r, NY)], drecv.at[half, r - 1], at_y(r))
+            d_cps[half][r] = remote(dsend.at[half, jnp.bitwise_and(y + r, NY - 1)], drecv.at[half, r - 1], at_y(r))
     ug_cps = []
     for r in range(1, NM):
         ug_cps.append(remote(ufin.at[m], ufin.at[m], at_m(r)))

time: 81.8 us -> 81.1 us (level)
  no operation moved by 1% of the time
where the time goes in v4:
time: 81.1 us; the launch traced here: 80.9 us
  Pallas kernels  80.3 us (99%)
    pallas_call x1, Pallas kernels, body(): pl.pallas_call(kernel, out_shape=(jax.ShapeDtypeStruct((432, 256), F32),...  79.4 us

profile of v4, /device:TPU:1, one launch (start us, length us, event | category | flops | bytes accessed | tf_op | source)
XLA Modules:
  0.0 80.9 jit_solution(1142630622694165916)
XLA Ops:
  0.6 79.4 %shard_map.139 = (f32[432,256]{1,0:T(8,128)S(1)}, f32[27,4,256]{2,1,0:T(4,128)S(1)}, f32[128,256]{1,0:T(8,128)S(1)}) custom-call(bf16[4096,256]{1,0:T(8,128)(2,1)} %bitcast.15, bf16[256,32]{1,0:T(8,128)(2,1)} %bitcast.18, bf16[27,16,256]{2,1,0:T(8,128)(2,1)} %bitcast.17, bf16[4,256,128]{2,1,0:T(8,128)(2,1)} %bitcast.16, ...), custom_call_target="tpu_custom_call" | custom-call | tf_op jit(solution)/shard_map/pallas_call | solution.py:499
  80.1 0.9 %shard_map.140 = (f32[432,256]{1,0:T(8,128)}, f32[27,4,256]{2,1,0:T(4,128)}, f32[128,256]{1,0:T(8,128)}) custom-call(f32[432,256]{1,0:T(8,128)S(1)} %get-tuple-element.9.a, f32[27,4,256]{2,1,0:T(4,128)S(1)} %get-tuple-element.10.b, f32[128,256]{1,0:T(8,128)S(1)} %get-tuple-element.11.c), custom_call_target="tpu_custom_call" | custom-call | tf_op jit(solution)/shard_map/pallas_call | solution.py:526

commit v5 on v4

--- a/solution.py
+++ b/solution.py
@@ -61,7 +61,7 @@
         for h in range(2):
             for y in range(8):
                 order[m * 16 + h * 8 + y, 4 * ((2 * (m % 2) + h) * 8 + y) + m // 2] = 1
-    pick = np.zeros((9, 512, 128), np.float32)
+    pick = np.zeros((5, 512, 256), np.float32)
     for j in range(3):
         for k in range(3):
             for z in range(2):
@@ -69,7 +69,7 @@
                     for x in range(8):
                         row, col = 2 * y + j - 1, 2 * x + k - 1
                         if row >= 0 and col >= 0:
-                            pick[j * 3 + k, z * 256 + row * 16 + col, z * 64 + y * 8 + x] = 1
+                            pick[(j * 3 + k) // 2, z * 256 + row * 16 + col, (j * 3 + k) % 2 * 128 + z * 64 + y * 8 + x] = 1
     return split, merge, spread16, shift, order, pick, np.eye(256, dtype=np.float32), np.tile(spread16, (16, 1))
 
 
@@ -135,16 +135,6 @@
         pending.append(cp)
         return cp
 
-    barrier = pltpu.get_barrier_semaphore()
-    partners = [at_y(d) for d in range(1, 8)] + [at_m(r) for r in range(1, 8)]
-    partners += [(s, lax.rem(ch + 1, 32)), (s, lax.rem(ch + 31, 32))]
-    for dzl in range(3):
-        for dzh in range(4):
-            if dzl or dzh:
-                partners.append(at_z(lax.rem(zl + dzl, 3), jnp.bitwise_and(zh + dzh, 3)))
-    for dev in partners:
-        pl.semaphore_signal(barrier, inc=1, device_id=dev, device_id_type=pl.DeviceIdType.MESH)
-
     loads = {}
     for i, (name, src, dst) in enumerate((
         ("f0", filt_hbm.at[:, :, 0:128], fbuf.at[0, 0, 0:27]), ("f1", filt_hbm.at[:, :, 128:256], fbuf.at[0, 1, 0:27]),
@@ -156,8 +146,30 @@
         cp = pltpu.make_async_copy(src, dst, load_sem.at[i])
         cp.start()
         loads[name] = cp
+    barrier = pltpu.get_barrier_semaphore()
+    partners = []
+    for dzh in (2, 1, 3, 0):
+        for dzl in range(3):
+            if dzl or dzh:
+                partners.append(at_z(lax.rem(zl + dzl, 3), jnp.bitwise_and(zh + dzh, 3)))
+    partners += [at_y(d) for d in (4, 3, 5, 2, 6, 1, 7)] + [at_m(r) for r in range(1, 8)]
+    partners += [(s, lax.rem(ch + 1, 32)), (s, lax.rem(ch + 31, 32))]
+    for dev in partners:
+        pl.semaphore_signal(barrier, inc=1, device_id=dev, device_id_type=pl.DeviceIdType.MESH)
+
     fbuf[0, :, 27] = jnp.zeros((2, 16, 128), BF)
 
+    for name in ("f0", "f1"):
+        loads[name].wait()
+
+    pl.semaphore_wait(barrier, len(partners))
+
+    share = pl.ds(7 * x, 7)
+    f_z = {}
+    for d in (2, 1, 3):
+        f_z[d] = remote(fbuf.at[0, c, share], fbuf.at[4 - d, c, share], at_zh(d))
+    loads["low"].wait()
+    rim_cp = remote(low_ref.at[3], rim, (s, lax.rem(ch + 1, 32)))
     loads["cot"].wait()
     loads["eye"].wait()
     planes[0:32, :] = lax.dot_general(
@@ -166,19 +178,9 @@
     planes[32:40, :] = jnp.zeros((8, 256), F32)
     for q in range(4):
         qsend[q] = planes[8 * q : 8 * q + 16, :].astype(BF)
-    for name in ("f0", "f1", "low"):
-        loads[name].wait()
-
-    pl.semaphore_wait(barrier, len(partners))
-
-    share = pl.ds(7 * x, 7)
-    f_z = {}
-    for d in (2, 1, 3):
-        f_z[d] = remote(fbuf.at[0, c, share], fbuf.at[4 - d, c, share], at_zh(d))
     q_cps = []
     for d in (2, 1, 3):
         q_cps.append(remote(qsend.at[jnp.bitwise_and(zh + d, NZH - 1)], qrecv.at[3 - d], at_zh(d)))
-    rim_cp = remote(low_ref.at[3], rim, (s, lax.rem(ch + 1, 32)))
 
     lane = lax.broadcasted_iota(jnp.int32, (128, 128), 1) // 16
 
@@ -198,17 +200,6 @@
     for g in range(4):
         w_ref[g] = shifted(wide_ref[128 * g : 128 * g + 128, :], wide_ref[128 * g + 16 : 128 * g + 144, :])
 
-    loads["split"].wait()
-    loads["act"].wait()
-
-    def split_group(g, carry):
-        got = mm(split_ref[...], act_ref[pl.ds(pl.multiple_of(g * 256, 256), 256), :]).astype(BF)
-        for p in range(8):
-            a_ref[p, pl.ds(pl.multiple_of(g * 32, 32), 32), :] = got[p * 32 : p * 32 + 32]
-        return carry
-
-    lax.fori_loop(0, 16, split_group, 0)
-
     f_x = {}
     f_c = {}
 
@@ -221,16 +212,6 @@
             cp.wait_recv()
         f_c[d] = remote(fbuf.at[4 - d, c], fbuf.at[4 - d, c], mate)
 
-    spread_x(1)
-    spread_x(3)
-
-    wt = jnp.concatenate([jnp.transpose(w_ref[g].astype(F32)) for g in range(4)], axis=1).astype(BF)
-    for p in range(8):
-        got = mm(wt, a_ref[p])
-        for q, tap in class_taps(p):
-            u_ref[tap * 16 : tap * 16 + 16, :] = got[q * 16 : q * 16 + 16]
-    u_ref[432:448, :] = jnp.zeros((16, 256), F32)
-    spread_x(2)
     loads["order"].wait()
     loads["pick"].wait()
     rim_cp.wait_recv()
@@ -243,26 +224,25 @@
     for i in range(3):
         lstack[i * 128 : i * 128 + 128, 0:256] = t_ref[i]
         lstack[i * 128 : i * 128 + 128, 256:512] = t_ref[i + 2]
-    spread_c(1)
-    spread_c(3)
-
-    def window(jk, carry):
-        got = mm(lstack[...], pick_ref[jk]).astype(BF)
+
+    def window(jj, taps):
+        got = mm(lstack[...], pick_ref[jj]).astype(BF)
         for i in range(3):
             for k in range(NM):
-                lsend[k, i * 9 + jk] = got[i * 128 + k * 16 : i * 128 + k * 16 + 16]
+                for tap in taps:
+                    rows = slice(i * 128 + k * 16, i * 128 + k * 16 + 16)
+                    lsend[k, i * 9 + 2 * jj + tap] = got[rows, 128 * tap : 128 * tap + 128]
+
+    def window_pair(jj, carry):
+        window(jj, (0, 1))
         return carry
 
-    lax.fori_loop(0, 9, window, 0)
-    spread_c(2)
-    u_cps = []
-    for r in range(1, NM):
-        u_cps.append(remote(u_ref.at[pl.ds(m_at(r) * PIECE, PIECE)], urecv.at[r - 1], at_m(r)))
-
-    l_cps = []
-    for r in range(1, NM):
-        l_cps.append(remote(lsend.at[m_at(r)], lrecv.at[m], at_m(r)))
-
+    lax.fori_loop(0, 2, window_pair, 0)
+    spread_x(1)
+    spread_x(3)
+    lax.fori_loop(2, 4, window_pair, 0)
+    window(4, (0,))
+    spread_x(2)
     loads["tall"].wait()
     for cp in q_cps:
         cp.wait_recv()
@@ -275,6 +255,13 @@
             wide_far[r, pl.ds(bc, 16, stride=16), :] = got[r * 16 : r * 16 + 16]
     for r in range(3):
         wq_ref[r + 1] = shifted(wide_far[r, 0:128, :], wide_far[r, 16:144, :])
+    spread_c(1)
+    spread_c(3)
+    spread_c(2)
+    l_cps = []
+    for r in range(1, NM):
+        l_cps.append(remote(lsend.at[m_at(r)], lrecv.at[m], at_m(r)))
+
     left = jnp.concatenate([wq_ref[r] for r in range(4)], axis=1)
     for d in (1, 3, 2):
         f_c[d].wait_recv()
@@ -313,21 +300,37 @@
                 part[o, quarters[u]] = part[o, quarters[u]] + rshort[t - 1, quarters[u]]
             shorts[t][u] = remote(part.at[o, quarters[u]], rshort.at[t, quarters[u]], at_y(back[u]))
 
+    def split_group(g, carry):
+        got = mm(split_ref[...], act_ref[pl.ds(pl.multiple_of(g * 256, 256), 256), :]).astype(BF)
+        for p in range(8):
+            a_ref[p, pl.ds(pl.multiple_of(g * 32, 32), 32), :] = got[p * 32 : p * 32 + 32]
+        return carry
+
+    def upper(p, wt):
+        got = mm(wt, a_ref[p])
+        for q, tap in class_taps(p):
+            u_ref[tap * 16 : tap * 16 + 16, :] = got[q * 16 : q * 16 + 16]
+
     for u in range(4):
         partial(2 * u)
         partial(2 * u + 1)
         ring(0, u)
-    for t in (1, 2):
-        for u in range(4):
-            ring(t, u)
-    piece = u_ref[pl.ds(pl.multiple_of(m * PIECE, 8), PIECE), :]
+    loads["split"].wait()
+    loads["act"].wait()
+    lax.fori_loop(0, 6, split_group, 0)
+    for u in range(4):
+        ring(1, u)
+        lax.fori_loop(6 + 3 * u, min(9 + 3 * u, 16), split_group, 0)
+    for u in range(4):
+        ring(2, u)
+        if u == 0:
+            wt = jnp.concatenate([jnp.transpose(w_ref[g].astype(F32)) for g in range(4)], axis=1).astype(BF)
+        upper(2 * u, wt)
+        upper(2 * u + 1, wt)
+    u_ref[432:448, :] = jnp.zeros((16, 256), F32)
+    u_cps = []
     for r in range(1, NM):
-        u_cps[r - 1].wait_recv()
-        piece = piece + urecv[r - 1]
-    uzl[zl] = piece
-    uz_cps = []
-    for d in (1, 2):
-        uz_cps.append(remote(uzl.at[zl], uzl.at[zl], at_z(lax.rem(zl + d, 3), zh)))
+        u_cps.append(remote(u_ref.at[pl.ds(m_at(r) * PIECE, PIECE)], urecv.at[r - 1], at_m(r)))
     for u in range(4):
         ring(3, u)
 
@@ -368,9 +371,14 @@
             c_x[h][r].wait_recv()
             got = from_x(r, c)
             c_f[h][r] = remote(call.at[got, h], call.at[got, h], mate)
-    for cp in uz_cps:
-        cp.wait_recv()
-    ufin[m] = (uzl[0] + uzl[1] + uzl[2]) * (1.0 / 24.0)
+    piece = u_ref[pl.ds(pl.multiple_of(m * PIECE, 8), PIECE), :]
+    for r in range(1, NM):
+        u_cps[r - 1].wait_recv()
+        piece = piece + urecv[r - 1]
+    uzl[zl] = piece
+    uz_cps = []
+    for d in (1, 2):
+        uz_cps.append(remote(uzl.at[zl], uzl.at[zl], at_z(lax.rem(zl + d, 3), zh)))
     acc = terms(c)
     for h in range(2):
         c_m[h].wait_recv()
@@ -388,6 +396,9 @@
             dsend[half, k] = jnp.concatenate([got, jnp.zeros((10, 128), BF)], axis=0)
         for r in (4, 3, 5, 2, 6, 1, 7):
             d_cps[half][r] = remote(dsend.at[half, jnp.bitwise_and(y + r, NY - 1)], drecv.at[half, r - 1], at_y(r))
+    for cp in uz_cps:
+        cp.wait_recv()
+    ufin[m] = (uzl[0] + uzl[1] + uzl[2]) * (1.0 / 24.0)
     ug_cps = []
     for r in range(1, NM):
         ug_cps.append(remote(ufin.at[m], ufin.at[m], at_m(r)))

time: 81.1 us -> 82.8 us (1.021)
  Pallas kernels: 80.3 us -> 82.1 us
    pallas_call x1, Pallas kernels: 79.4 us -> 81.2 us  [body(): pl.pallas_call(kernel, out_shape=(jax.ShapeDtypeStruct((432, 256), F32),...]
where the time goes in v5:
time: 82.8 us; the launch traced here: 82.7 us
  Pallas kernels  82.1 us (99%)
    pallas_call x1, Pallas kernels, body(): pl.pallas_call(kernel, out_shape=(jax.ShapeDtypeStruct((432, 256), F32),...  81.2 us

profile of v5, /device:TPU:1, one launch (start us, length us, event | category | flops | bytes accessed | tf_op | source)
XLA Modules:
  0.0 82.7 jit_solution(13127673873381988418)
XLA Ops:
  0.6 81.2 %shard_map.139 = (f32[432,256]{1,0:T(8,128)S(1)}, f32[27,4,256]{2,1,0:T(4,128)S(1)}, f32[128,256]{1,0:T(8,128)S(1)}) custom-call(bf16[4096,256]{1,0:T(8,128)(2,1)} %bitcast.15, bf16[256,32]{1,0:T(8,128)(2,1)} %bitcast.18, bf16[27,16,256]{2,1,0:T(8,128)(2,1)} %bitcast.17, bf16[4,256,128]{2,1,0:T(8,128)(2,1)} %bitcast.16, ...), custom_call_target="tpu_custom_call" | custom-call | tf_op jit(solution)/shard_map/pallas_call | solution.py:510
  81.8 0.9 %shard_map.140 = (f32[432,256]{1,0:T(8,128)}, f32[27,4,256]{2,1,0:T(4,128)}, f32[128,256]{1,0:T(8,128)}) custom-call(f32[432,256]{1,0:T(8,128)S(1)} %get-tuple-element.9.a, f32[27,4,256]{2,1,0:T(4,128)S(1)} %get-tuple-element.10.b, f32[128,256]{1,0:T(8,128)S(1)} %get-tuple-element.11.c), custom_call_target="tpu_custom_call" | custom-call | tf_op jit(solution)/shard_map/pallas_call | solution.py:537

commit v6 on v5

--- a/solution.py
+++ b/solution.py
@@ -159,17 +159,6 @@
 
     fbuf[0, :, 27] = jnp.zeros((2, 16, 128), BF)
 
-    for name in ("f0", "f1"):
-        loads[name].wait()
-
-    pl.semaphore_wait(barrier, len(partners))
-
-    share = pl.ds(7 * x, 7)
-    f_z = {}
-    for d in (2, 1, 3):
-        f_z[d] = remote(fbuf.at[0, c, share], fbuf.at[4 - d, c, share], at_zh(d))
-    loads["low"].wait()
-    rim_cp = remote(low_ref.at[3], rim, (s, lax.rem(ch + 1, 32)))
     loads["cot"].wait()
     loads["eye"].wait()
     planes[0:32, :] = lax.dot_general(
@@ -178,6 +167,17 @@
     planes[32:40, :] = jnp.zeros((8, 256), F32)
     for q in range(4):
         qsend[q] = planes[8 * q : 8 * q + 16, :].astype(BF)
+    for name in ("f0", "f1"):
+        loads[name].wait()
+
+    pl.semaphore_wait(barrier, len(partners))
+
+    share = pl.ds(7 * x, 7)
+    f_z = {}
+    for d in (2, 1, 3):
+        f_z[d] = remote(fbuf.at[0, c, share], fbuf.at[4 - d, c, share], at_zh(d))
+    loads["low"].wait()
+    rim_cp = remote(low_ref.at[3], rim, (s, lax.rem(ch + 1, 32)))
     q_cps = []
     for d in (2, 1, 3):
         q_cps.append(remote(qsend.at[jnp.bitwise_and(zh + d, NZH - 1)], qrecv.at[3 - d], at_zh(d)))
@@ -188,17 +188,6 @@
         both = jnp.where(lane >= 4, far, near)
         terms = [jnp.where(lane % 4 == k, both, 0.0).astype(BF) for k in range(4)]
         return mm(shift_ref[...], jnp.concatenate(terms, axis=0)).astype(BF)
-
-    loads["spread"].wait()
-    loads["shift"].wait()
-    for bc in range(16):
-        got = lax.dot_general(
-            cot_ref[bc * 16 : bc * 16 + 16, :], spread_ref[...], (((0,), (0,)), ((), ())), preferred_element_type=F32
-        )
-        wide_ref[pl.ds(bc, 32, stride=16), :] = got
-    wide_ref[512:528, :] = jnp.zeros((16, 128), F32)
-    for g in range(4):
-        w_ref[g] = shifted(wide_ref[128 * g : 128 * g + 128, :], wide_ref[128 * g + 16 : 128 * g + 144, :])
 
     f_x = {}
     f_c = {}
@@ -237,6 +226,15 @@
         window(jj, (0, 1))
         return carry
 
+    loads["split"].wait()
+    loads["act"].wait()
+
+    def split_group(g, carry):
+        got = mm(split_ref[...], act_ref[pl.ds(pl.multiple_of(g * 256, 256), 256), :]).astype(BF)
+        for p in range(8):
+            a_ref[p, pl.ds(pl.multiple_of(g * 32, 32), 32), :] = got[p * 32 : p * 32 + 32]
+        return carry
+
     lax.fori_loop(0, 2, window_pair, 0)
     spread_x(1)
     spread_x(3)
@@ -244,24 +242,27 @@
     window(4, (0,))
     spread_x(2)
     loads["tall"].wait()
+    loads["shift"].wait()
     for cp in q_cps:
         cp.wait_recv()
-    wq_ref[0] = w_ref[zh]
-    group = lax.broadcasted_iota(jnp.int32, (48, 256), 1) // 16
-    rows = jnp.concatenate([qrecv[0], qrecv[1], qrecv[2]], axis=0).astype(F32)
+    group = lax.broadcasted_iota(jnp.int32, (64, 256), 1) // 16
+    rows = jnp.concatenate([qsend[zh], qrecv[0], qrecv[1], qrecv[2]], axis=0).astype(F32)
     for bc in range(16):
         got = mm(jnp.where(group == bc, rows, 0.0).astype(BF), tall_ref[...])
-        for r in range(3):
+        for r in range(4):
             wide_far[r, pl.ds(bc, 16, stride=16), :] = got[r * 16 : r * 16 + 16]
-    for r in range(3):
-        wq_ref[r + 1] = shifted(wide_far[r, 0:128, :], wide_far[r, 16:144, :])
+    for r in range(4):
+        wq_ref[r] = shifted(wide_far[r, 0:128, :], wide_far[r, 16:144, :])
+    lax.fori_loop(0, 6, split_group, 0)
     spread_c(1)
     spread_c(3)
+    lax.fori_loop(6, 10, split_group, 0)
     spread_c(2)
     l_cps = []
     for r in range(1, NM):
         l_cps.append(remote(lsend.at[m_at(r)], lrecv.at[m], at_m(r)))
 
+    lax.fori_loop(10, 16, split_group, 0)
     left = jnp.concatenate([wq_ref[r] for r in range(4)], axis=1)
     for d in (1, 3, 2):
         f_c[d].wait_recv()
@@ -300,12 +301,6 @@
                 part[o, quarters[u]] = part[o, quarters[u]] + rshort[t - 1, quarters[u]]
             shorts[t][u] = remote(part.at[o, quarters[u]], rshort.at[t, quarters[u]], at_y(back[u]))
 
-    def split_group(g, carry):
-        got = mm(split_ref[...], act_ref[pl.ds(pl.multiple_of(g * 256, 256), 256), :]).astype(BF)
-        for p in range(8):
-            a_ref[p, pl.ds(pl.multiple_of(g * 32, 32), 32), :] = got[p * 32 : p * 32 + 32]
-        return carry
-
     def upper(p, wt):
         got = mm(wt, a_ref[p])
         for q, tap in class_taps(p):
@@ -315,22 +310,30 @@
         partial(2 * u)
         partial(2 * u + 1)
         ring(0, u)
-    loads["split"].wait()
-    loads["act"].wait()
-    lax.fori_loop(0, 6, split_group, 0)
+    loads["spread"].wait()
     for u in range(4):
         ring(1, u)
-        lax.fori_loop(6 + 3 * u, min(9 + 3 * u, 16), split_group, 0)
-    for u in range(4):
-        ring(2, u)
         if u == 0:
+            for bc in range(16):
+                got = lax.dot_general(
+                    cot_ref[bc * 16 : bc * 16 + 16, :], spread_ref[...], (((0,), (0,)), ((), ())),
+                    preferred_element_type=F32,
+                )
+                wide_ref[pl.ds(bc, 32, stride=16), :] = got
+            wide_ref[512:528, :] = jnp.zeros((16, 128), F32)
+        if u == 1:
+            for g in range(4):
+                w_ref[g] = shifted(wide_ref[128 * g : 128 * g + 128, :], wide_ref[128 * g + 16 : 128 * g + 144, :])
             wt = jnp.concatenate([jnp.transpose(w_ref[g].astype(F32)) for g in range(4)], axis=1).astype(BF)
-        upper(2 * u, wt)
-        upper(2 * u + 1, wt)
+        if u > 1:
+            for p in range(4 * u - 8, 4 * u - 4):
+                upper(p, wt)
     u_ref[432:448, :] = jnp.zeros((16, 256), F32)
     u_cps = []
     for r in range(1, NM):
         u_cps.append(remote(u_ref.at[pl.ds(m_at(r) * PIECE, PIECE)], urecv.at[r - 1], at_m(r)))
+    for u in range(4):
+        ring(2, u)
     for u in range(4):
         ring(3, u)
 
@@ -371,14 +374,6 @@
             c_x[h][r].wait_recv()
             got = from_x(r, c)
             c_f[h][r] = remote(call.at[got, h], call.at[got, h], mate)
-    piece = u_ref[pl.ds(pl.multiple_of(m * PIECE, 8), PIECE), :]
-    for r in range(1, NM):
-        u_cps[r - 1].wait_recv()
-        piece = piece + urecv[r - 1]
-    uzl[zl] = piece
-    uz_cps = []
-    for d in (1, 2):
-        uz_cps.append(remote(uzl.at[zl], uzl.at[zl], at_z(lax.rem(zl + d, 3), zh)))
     acc = terms(c)
     for h in range(2):
         c_m[h].wait_recv()
@@ -396,13 +391,14 @@
             dsend[half, k] = jnp.concatenate([got, jnp.zeros((10, 128), BF)], axis=0)
         for r in (4, 3, 5, 2, 6, 1, 7):
             d_cps[half][r] = remote(dsend.at[half, jnp.bitwise_and(y + r, NY - 1)], drecv.at[half, r - 1], at_y(r))
-    for cp in uz_cps:
-        cp.wait_recv()
-    ufin[m] = (uzl[0] + uzl[1] + uzl[2]) * (1.0 / 24.0)
-    ug_cps = []
+    piece = u_ref[pl.ds(pl.multiple_of(m * PIECE, 8), PIECE), :]
     for r in range(1, NM):
-        ug_cps.append(remote(ufin.at[m], ufin.at[m], at_m(r)))
-
+        u_cps[r - 1].wait_recv()
+        piece = piece + urecv[r - 1]
+    uzl[zl] = piece
+    uz_cps = []
+    for d in (1, 2):
+        uz_cps.append(remote(uzl.at[zl], uzl.at[zl], at_z(lax.rem(zl + d, 3), zh)))
     myz = zh * 3 + zl
     home = zh // 2 == c
     zbase = counter[0]
@@ -431,11 +427,12 @@
                 pl.when(away)(cp.start)
                 zsends.append((away, cp))
 
-    for cp in ug_cps:
+    for cp in uz_cps:
         cp.wait_recv()
-    for k in range(NM):
-        rows = min(PIECE, 432 - k * PIECE)
-        out_up[k * PIECE : k * PIECE + rows, :] = ufin[k, 0:rows]
+    ufin[m] = (uzl[0] + uzl[1] + uzl[2]) * (1.0 / 24.0)
+    ug_cps = []
+    for r in range(1, NM):
+        ug_cps.append(remote(ufin.at[m], ufin.at[m], at_m(r)))
 
     xbase = counter[0]
     counter[0] += 2 * NX
@@ -471,6 +468,11 @@
             )
             pl.when(home)(cp.start)
             xsends.append(cp)
+    for cp in ug_cps:
+        cp.wait_recv()
+    for k in range(NM):
+        rows = min(PIECE, 432 - k * PIECE)
+        out_up[k * PIECE : k * PIECE + rows, :] = ufin[k, 0:rows]
     for half in range(2):
         for k in range(NX):
             cp = pltpu.make_async_remote_copy(
@@ -519,7 +521,7 @@
         scratch_shapes=[
             vm(act.shape, BF), vm(cot.shape, BF), vm((4, 2, 28, 16, 128), BF), vm(low.shape, BF),
             *[vm(t.shape, t.dtype) for t in consts],
-            vm((528, 128), F32), vm((3, 256, 128), F32), vm((40, 256), F32), vm((4, 16, 256), BF), vm((3, 16, 256), BF),
+            vm((528, 128), F32), vm((4, 256, 128), F32), vm((40, 256), F32), vm((4, 16, 256), BF), vm((3, 16, 256), BF),
             vm((4, 128, 128), BF), vm((4, 128, 128), BF), vm((8, 512, 256), BF),
             vm((448, 256), F32), vm((7, PIECE, 256), F32), vm((3, PIECE, 256), F32), vm((NM, PIECE, 256), F32),
             vm((2, 512, 256), BF), vm((8, 8, 16, 256), F32), vm((4, 8, 16, 256), F32), vm((3, 8, 16, 256), F32),

time: 82.8 us -> 83.4 us (level)
  no operation moved by 1% of the time
where the time goes in v6:
time: 83.4 us; the launch traced here: 83.2 us
  Pallas kernels  82.6 us (99%)
    pallas_call x1, Pallas kernels, body(): pl.pallas_call(kernel, out_shape=(jax.ShapeDtypeStruct((432, 256), F32),...  81.7 us

profile of v6, /device:TPU:1, one launch (start us, length us, event | category | flops | bytes accessed | tf_op | source)
XLA Modules:
  0.0 83.2 jit_solution(12528040794110063109)
XLA Ops:
  0.6 81.7 %shard_map.139 = (f32[432,256]{1,0:T(8,128)S(1)}, f32[27,4,256]{2,1,0:T(4,128)S(1)}, f32[128,256]{1,0:T(8,128)S(1)}) custom-call(bf16[4096,256]{1,0:T(8,128)(2,1)} %bitcast.15, bf16[256,32]{1,0:T(8,128)(2,1)} %bitcast.18, bf16[27,16,256]{2,1,0:T(8,128)(2,1)} %bitcast.17, bf16[4,256,128]{2,1,0:T(8,128)(2,1)} %bitcast.16, ...), custom_call_target="tpu_custom_call" | custom-call | tf_op jit(solution)/shard_map/pallas_call | solution.py:512
  82.4 0.9 %shard_map.140 = (f32[432,256]{1,0:T(8,128)}, f32[27,4,256]{2,1,0:T(4,128)}, f32[128,256]{1,0:T(8,128)}) custom-call(f32[432,256]{1,0:T(8,128)S(1)} %get-tuple-element.9.a, f32[27,4,256]{2,1,0:T(4,128)S(1)} %get-tuple-element.10.b, f32[128,256]{1,0:T(8,128)S(1)} %get-tuple-element.11.c), custom_call_target="tpu_custom_call" | custom-call | tf_op jit(solution)/shard_map/pallas_call | solution.py:539

commit v7 on v4

--- a/solution.py
+++ b/solution.py
@@ -61,7 +61,7 @@
         for h in range(2):
             for y in range(8):
                 order[m * 16 + h * 8 + y, 4 * ((2 * (m % 2) + h) * 8 + y) + m // 2] = 1
-    pick = np.zeros((9, 512, 128), np.float32)
+    pick = np.zeros((5, 512, 256), np.float32)
     for j in range(3):
         for k in range(3):
             for z in range(2):
@@ -69,7 +69,7 @@
                     for x in range(8):
                         row, col = 2 * y + j - 1, 2 * x + k - 1
                         if row >= 0 and col >= 0:
-                            pick[j * 3 + k, z * 256 + row * 16 + col, z * 64 + y * 8 + x] = 1
+                            pick[(j * 3 + k) // 2, z * 256 + row * 16 + col, (j * 3 + k) % 2 * 128 + z * 64 + y * 8 + x] = 1
     return split, merge, spread16, shift, order, pick, np.eye(256, dtype=np.float32), np.tile(spread16, (16, 1))
 
 
@@ -243,26 +243,6 @@
     for i in range(3):
         lstack[i * 128 : i * 128 + 128, 0:256] = t_ref[i]
         lstack[i * 128 : i * 128 + 128, 256:512] = t_ref[i + 2]
-    spread_c(1)
-    spread_c(3)
-
-    def window(jk, carry):
-        got = mm(lstack[...], pick_ref[jk]).astype(BF)
-        for i in range(3):
-            for k in range(NM):
-                lsend[k, i * 9 + jk] = got[i * 128 + k * 16 : i * 128 + k * 16 + 16]
-        return carry
-
-    lax.fori_loop(0, 9, window, 0)
-    spread_c(2)
-    u_cps = []
-    for r in range(1, NM):
-        u_cps.append(remote(u_ref.at[pl.ds(m_at(r) * PIECE, PIECE)], urecv.at[r - 1], at_m(r)))
-
-    l_cps = []
-    for r in range(1, NM):
-        l_cps.append(remote(lsend.at[m_at(r)], lrecv.at[m], at_m(r)))
-
     loads["tall"].wait()
     for cp in q_cps:
         cp.wait_recv()
@@ -275,6 +255,33 @@
             wide_far[r, pl.ds(bc, 16, stride=16), :] = got[r * 16 : r * 16 + 16]
     for r in range(3):
         wq_ref[r + 1] = shifted(wide_far[r, 0:128, :], wide_far[r, 16:144, :])
+    spread_c(1)
+    spread_c(3)
+
+    def window(jj, taps):
+        got = mm(lstack[...], pick_ref[jj]).astype(BF)
+        for i in range(3):
+            for k in range(NM):
+                for tap in taps:
+                    rows = slice(i * 128 + k * 16, i * 128 + k * 16 + 16)
+                    lsend[k, i * 9 + 2 * jj + tap] = got[rows, 128 * tap : 128 * tap + 128]
+
+    def window_pair(jj, carry):
+        window(jj, (0, 1))
+        return carry
+
+    lax.fori_loop(0, 2, window_pair, 0)
+    spread_c(2)
+    u_cps = []
+    for r in range(1, NM):
+        u_cps.append(remote(u_ref.at[pl.ds(m_at(r) * PIECE, PIECE)], urecv.at[r - 1], at_m(r)))
+
+    lax.fori_loop(2, 4, window_pair, 0)
+    window(4, (0,))
+    l_cps = []
+    for r in range(1, NM):
+        l_cps.append(remote(lsend.at[m_at(r)], lrecv.at[m], at_m(r)))
+
     left = jnp.concatenate([wq_ref[r] for r in range(4)], axis=1)
     for d in (1, 3, 2):
         f_c[d].wait_recv()

time: 81.1 us -> 80 us (0.986)
  Pallas kernels: 80.3 us -> 79.2 us
    pallas_call x1, Pallas kernels: 79.4 us -> 78.3 us  [body(): pl.pallas_call(kernel, out_shape=(jax.ShapeDtypeStruct((432, 256), F32),...]
where the time goes in v7:
time: 80 us; the launch traced here: 79.8 us
  Pallas kernels  79.2 us (99%)
    pallas_call x1, Pallas kernels, body(): pl.pallas_call(kernel, out_shape=(jax.ShapeDtypeStruct((432, 256), F32),...  78.3 us

profile of v7, /device:TPU:1, one launch (start us, length us, event | category | flops | bytes accessed | tf_op | source)
XLA Modules:
  0.0 79.8 jit_solution(14570031747228301778)
XLA Ops:
  0.6 78.3 %shard_map.139 = (f32[432,256]{1,0:T(8,128)S(1)}, f32[27,4,256]{2,1,0:T(4,128)S(1)}, f32[128,256]{1,0:T(8,128)S(1)}) custom-call(bf16[4096,256]{1,0:T(8,128)(2,1)} %bitcast.15, bf16[256,32]{1,0:T(8,128)(2,1)} %bitcast.18, bf16[27,16,256]{2,1,0:T(8,128)(2,1)} %bitcast.17, bf16[4,256,128]{2,1,0:T(8,128)(2,1)} %bitcast.16, ...), custom_call_target="tpu_custom_call" | custom-call | tf_op jit(solution)/shard_map/pallas_call | solution.py:506
  79.0 0.9 %shard_map.140 = (f32[432,256]{1,0:T(8,128)}, f32[27,4,256]{2,1,0:T(4,128)}, f32[128,256]{1,0:T(8,128)}) custom-call(f32[432,256]{1,0:T(8,128)S(1)} %get-tuple-element.9.a, f32[27,4,256]{2,1,0:T(4,128)S(1)} %get-tuple-element.10.b, f32[128,256]{1,0:T(8,128)S(1)} %get-tuple-element.11.c), custom_call_target="tpu_custom_call" | custom-call | tf_op jit(solution)/shard_map/pallas_call | solution.py:533
